TPU v7x, 1024 devices: a whole 4x4x32 slice. The times are simulated.
1024 devices in a mesh: region: 8 (over y_hi, x), dom: 128 (over y_lo, z, core).
Axes of the slice: x: 4, y: 4 (y_hi: 2, y_lo: 2; y = y_hi * 2 + y_lo), z: 32, core: 2. Of those that a mesh axis runs over, the one named last changes fastest.
Arguments:
- displacement: float32 [3, 1048576], P(None, ('region', 'dom')), may hold values from -6 to 6
- velocity: float32 [3, 1048576], P(None, ('region', 'dom')), may hold values from -6 to 6
- acceleration: float32 [3, 1048576], P(None, ('region', 'dom')), may hold values from -6 to 6
- solid_mass_inverse: float32 [1048576], P(('region', 'dom')), may hold values from 0.05 to 0.3
- connectivity: int32 [125, 32768], P(None, ('region', 'dom')), may hold values from 0 to 1023
- lame_lambda: bfloat16 [125, 32768], P(None, ('region', 'dom')), may hold values from 0.5 to 2
- shear_modulus: bfloat16 [125, 32768], P(None, ('region', 'dom')), may hold values from 0.29882812 to 1.5
- inverse_size: float32 [32768], P(('region', 'dom')), may hold values from 0.7 to 1.4
- potential: float32 [524288], P(('region', 'dom')), may hold values from -6 to 6
- potential_dot: float32 [524288], P(('region', 'dom')), may hold values from -6 to 6
- potential_ddot: float32 [524288], P(('region', 'dom')), may hold values from -6 to 6
- fluid_mass_inverse: float32 [524288], P(('region', 'dom')), may hold values from 0.1 to 0.5
- fluid_connectivity: int32 [125, 16384], P(None, ('region', 'dom')), may hold values from 0 to 511
- density_inverse: bfloat16 [125, 16384], P(None, ('region', 'dom')), may hold values from 0.5 to 2
- fluid_inverse_size: float32 [16384], P(('region', 'dom')), may hold values from 0.7 to 1.4
- solid_halo: int32 [2, 98304], P(None, ('region', 'dom')), may hold values from 0 to 1023, as said below
- fluid_halo: int32 [2, 49152], P(None, ('region', 'dom')), may hold values from 0 to 511, as said below
- solid_interface: int32 [2, 1048576], P(None, ('region', 'dom')), may hold values from -1 to 1023, as said below
- fluid_interface: int32 [2, 1048576], P(None, ('region', 'dom')), may hold values from -1 to 511, as said below
- interface_normal: float32 [3, 2, 1048576], P(None, None, ('region', 'dom')), may hold values from -6 to 6
Outputs:
- velocity_new: float32 [3, 1048576], P(None, ('region', 'dom'))
- acceleration_new: float32 [3, 1048576], P(None, ('region', 'dom'))
- potential_dot_new: float32 [524288], P(('region', 'dom'))
- potential_ddot_new: float32 [524288], P(('region', 'dom'))
Inputs may be any that keep to these rules, and one draw needn't show every extreme that they name: `solid_halo`: on each partition the 96 nodes of row 0 and of row 1 are all different. Column k of row 1 on dom index d and column k of row 0 on dom index d + 1 (cyclically, same region index) name one node shared by the two partitions. `fluid_halo`: on each partition the 48 nodes of row 0 and of row 1 are all different. Column k of row 1 on dom index d and column k of row 0 on dom index d + 1 (cyclically, same region index) name one node shared by the two partitions. -1 marks an empty slot, and the live slots of each row come first. Slot k of row 1 on partition (r, d) pairs with slot k of row 0 of fluid_interface on partition (r + 1, d), and slot k of row 0 on (r, d) with slot k of row 1 of fluid_interface on (r - 1, d); both are live or both empty. Row 0 of region index 0 and row 1 of region index 7 are empty; every other row holds more than half of 1024 live slots. For every region index r below 7 and every dom index, row 1 of solid_interface on (r, d) or row 1 of fluid_interface on (r, d) is full (1024 live slots). A node may stand in several slots. `fluid_interface`: -1 marks an empty slot, and the live slots of each row come first; pairing as stated for solid_interface. Row 0 of region index 0 and row 1 of region index 7 are empty; every other row holds more than half of 1024 live slots.
All inputs are finite; a program needn't handle non-finite values.
Results may differ from a plain program's by a relative error of at most 0.0003.
Values sent between devices are 32-bit elements; how exact they have to be, the bound alone decides.
A program may use at most 32 MiB of HBM per device.

v0:
```python
import math

import jax
import jax.numpy as jnp
import numpy as np
from jax import lax
from jax.sharding import PartitionSpec as P

time_step = 0.4


def extended(cells, sides, width, closed):
    for axis, dim in sides:
        count = lax.axis_size(axis)
        ends = count if closed else count - 1
        head = lax.slice_in_dim(cells, 0, width, axis=dim)
        tail = lax.slice_in_dim(cells, cells.shape[dim] - width, cells.shape[dim], axis=dim)
        cells = jnp.concatenate(
            [
                lax.ppermute(tail, axis, [(i, (i + 1) % count) for i in range(ends)]),
                cells,
                lax.ppermute(head, axis, [((i + 1) % count, i) for i in range(ends)]),
            ],
            axis=dim,
        )
    return cells


def gll_tables():
    points = np.array([-1.0, -math.sqrt(3.0 / 7.0), 0.0, math.sqrt(3.0 / 7.0), 1.0])
    weights = np.array([0.1, 49.0 / 90.0, 32.0 / 45.0, 49.0 / 90.0, 0.1])
    products = np.array(
        [
            np.prod(
                [points[row_index] - points[column] for column in range(5) if column != row_index]
            )
            for row_index in range(5)
        ]
    )
    derivative = np.zeros((5, 5))
    for row_index in range(5):
        for col_index in range(5):
            if row_index != col_index:
                derivative[row_index, col_index] = products[row_index] / (
                    products[col_index] * (points[row_index] - points[col_index])
                )
            else:
                derivative[row_index, col_index] = sum(
                    (
                        1.0 / (points[row_index] - points[column])
                        for column in range(5)
                        if column != row_index
                    )
                )
    weight_cube = weights[:, None, None] * weights[None, :, None] * weights[None, None, :]
    return (jnp.asarray(derivative, jnp.float32), jnp.asarray(weight_cube, jnp.float32))


def derivatives_of(derivative, values):
    highest = lax.Precision.HIGHEST
    along_first = jnp.einsum("il,...ljke->...ijke", derivative, values, precision=highest)
    along_second = jnp.einsum("jl,...ilke->...ijke", derivative, values, precision=highest)
    along_third = jnp.einsum("kl,...ijle->...ijke", derivative, values, precision=highest)
    return (along_first, along_second, along_third)


def divergence_of(derivative, along_first, along_second, along_third):
    highest = lax.Precision.HIGHEST
    return (
        jnp.einsum("il,...ijke->...ljke", derivative, along_first, precision=highest)
        + jnp.einsum("jl,...ijke->...ilke", derivative, along_second, precision=highest)
        + jnp.einsum("kl,...ijke->...ijle", derivative, along_third, precision=highest)
    )


def solid_element_forces(
    displaced, connectivity, lame_lambda, shear_modulus, inverse_size, derivative, weight_cube
):
    element_count = connectivity.shape[1]
    node_count = displaced.shape[1]
    local_values = displaced[:, connectivity].reshape(3, 5, 5, 5, element_count)
    gradient = jnp.stack(derivatives_of(derivative, local_values), axis=1) * inverse_size
    lame_values = lame_lambda.astype(jnp.float32).reshape(5, 5, 5, element_count)
    shear_values = shear_modulus.astype(jnp.float32).reshape(5, 5, 5, element_count)
    trace_value = gradient[0, 0] + gradient[1, 1] + gradient[2, 2]
    identity = jnp.eye(3, dtype=jnp.float32)[:, :, None, None, None, None]
    stress = lame_values * trace_value * identity + shear_values * (
        gradient + jnp.swapaxes(gradient, 0, 1)
    )
    weighted = stress * (weight_cube[:, :, :, None] / (inverse_size * inverse_size))
    element_force = -divergence_of(derivative, weighted[:, 0], weighted[:, 1], weighted[:, 2])
    return (
        jnp.zeros((3, node_count), jnp.float32)
        .at[:, connectivity]
        .add(element_force.reshape(3, 125, element_count))
    )


def fluid_element_forces(
    potential_values, connectivity, density_inverse, inverse_size, derivative, weight_cube
):
    element_count = connectivity.shape[1]
    node_count = potential_values.shape[0]
    local_values = potential_values[connectivity].reshape(5, 5, 5, element_count)
    gradient = jnp.stack(derivatives_of(derivative, local_values), axis=0) * inverse_size
    factor = (
        weight_cube[:, :, :, None]
        * density_inverse.astype(jnp.float32).reshape(5, 5, 5, element_count)
        / (inverse_size * inverse_size)
    )
    weighted = gradient * factor
    element_force = -divergence_of(derivative, weighted[0], weighted[1], weighted[2])
    return (
        jnp.zeros((node_count,), jnp.float32)
        .at[connectivity]
        .add(element_force.reshape(125, element_count))
    )


def on_device(
    displacement,
    velocity,
    acceleration,
    solid_mass_inverse,
    connectivity,
    lame_lambda,
    shear_modulus,
    inverse_size,
    potential,
    potential_dot,
    potential_ddot,
    fluid_mass_inverse,
    fluid_connectivity,
    density_inverse,
    fluid_inverse_size,
    solid_halo,
    fluid_halo,
    solid_interface,
    fluid_interface,
    interface_normal,
):
    derivative, weight_cube = gll_tables()
    half_square = 0.5 * time_step * time_step
    predicted = displacement + time_step * velocity + half_square * acceleration
    fluid_predicted = potential + time_step * potential_dot + half_square * potential_ddot
    solid_live = solid_interface >= 0
    fluid_live = fluid_interface >= 0
    solid_target = jnp.where(solid_live, solid_interface, displacement.shape[1])
    fluid_target = jnp.where(fluid_live, fluid_interface, potential.shape[0])
    gathered_motion = predicted[:, jnp.where(solid_live, solid_interface, 0)]
    normal_motion = jnp.where(solid_live, jnp.sum(interface_normal * gathered_motion, axis=0), 0.0)
    motion_padded = extended(normal_motion, (("region", 0),), 1, False)
    arrived_motion = jnp.stack([motion_padded[0], motion_padded[3]])
    fluid_force = fluid_element_forces(
        fluid_predicted,
        fluid_connectivity,
        density_inverse,
        fluid_inverse_size,
        derivative,
        weight_cube,
    )
    fluid_force = fluid_force.at[fluid_target].add(arrived_motion, mode="drop")
    fluid_rim = jnp.stack([fluid_force[fluid_halo[0]], fluid_force[fluid_halo[1]]])
    fluid_padded = extended(fluid_rim, (("dom", 0),), 1, True)
    fluid_force = (
        fluid_force.at[fluid_halo[0]].add(fluid_padded[0]).at[fluid_halo[1]].add(fluid_padded[3])
    )
    potential_ddot_new = fluid_mass_inverse * fluid_force
    potential_dot_new = potential_dot + 0.5 * time_step * (potential_ddot + potential_ddot_new)
    boundary_pressure = jnp.where(
        fluid_live, potential_ddot_new[jnp.where(fluid_live, fluid_interface, 0)], 0.0
    )
    pressure_padded = extended(boundary_pressure, (("region", 0),), 1, False)
    arrived_pressure = jnp.stack([pressure_padded[0], pressure_padded[3]])
    coupling_force = (
        jnp.zeros(displacement.shape, jnp.float32)
        .at[:, solid_target]
        .add(-interface_normal * arrived_pressure, mode="drop")
    )
    element_force = solid_element_forces(
        predicted, connectivity, lame_lambda, shear_modulus, inverse_size, derivative, weight_cube
    )
    solid_total = element_force + coupling_force
    solid_rim = jnp.stack([solid_total[:, solid_halo[0]], solid_total[:, solid_halo[1]]])
    solid_padded = extended(solid_rim, (("dom", 0),), 1, True)
    solid_total = (
        solid_total.at[:, solid_halo[0]]
        .add(solid_padded[0])
        .at[:, solid_halo[1]]
        .add(solid_padded[3])
    )
    acceleration_new = solid_mass_inverse * solid_total
    velocity_new = velocity + 0.5 * time_step * (acceleration + acceleration_new)
    return (velocity_new, acceleration_new, potential_dot_new, potential_ddot_new)


def solution(mesh):
    in_specs = (
        P(None, ("region", "dom")),
        P(None, ("region", "dom")),
        P(None, ("region", "dom")),
        P(("region", "dom")),
        P(None, ("region", "dom")),
        P(None, ("region", "dom")),
        P(None, ("region", "dom")),
        P(("region", "dom")),
        P(("region", "dom")),
        P(("region", "dom")),
        P(("region", "dom")),
        P(("region", "dom")),
        P(None, ("region", "dom")),
        P(None, ("region", "dom")),
        P(("region", "dom")),
        P(None, ("region", "dom")),
        P(None, ("region", "dom")),
        P(None, ("region", "dom")),
        P(None, ("region", "dom")),
        P(None, None, ("region", "dom")),
    )
    out_specs = (
        P(None, ("region", "dom")),
        P(None, ("region", "dom")),
        P(("region", "dom")),
        P(("region", "dom")),
    )
    return jax.shard_map(
        on_device, mesh=mesh, in_specs=in_specs, out_specs=out_specs, check_vma=False
    )
```

profile of v0, /device:TPU:6, one launch (start us, length us, event | category | flops | bytes accessed | tf_op | source)
XLA Modules:
  0.0 175.1 jit_solution(13756296723374426101)
XLA Ops:
  0.7 0.8 multiply_add_fusion.1
  1.5 0.2 copy.159
  1.7 0.7 fusion.36
  2.4 5.5 %gather_fusion.2 = f32[2048,3]{1,0:T(8,128)S(1)} fusion(f32[3,1024]{0,1:T(8,128)S(1)} %copy.159, s32[2048]{0:T(1024)S(1)} %bitcast_clamp_fusion.1), kind=kCustom, calls=%fused_computation.2 | custom fusion | bytes 57344 | tf_op jit(solution)/shard_map/gather | solution.py:150
  7.9 0.3 copy.195
  8.2 0.8 fusion.33
  9.0 0.7 compare_select_fusion.9
  9.7 5.0 %collective-permute-start = (f32[1,1024]{1,0:T(1,128)S(1)}, f32[1,1024]{1,0:T(1,128)S(1)}, u32[]{:S(2)}, u32[]{:S(2)}) collective-permute-start(f32[1,1024]{1,0:T(1,128)S(1)} %get-tuple-element.32), channel_id=1, source_target_pairs={{0,128},{128,256},{256,384},{384,512},{512,640},{640,768},{768,896... | collective-permute-start | bytes 12296 | tf_op jit(solution)/shard_map/ppermute | solution.py:20
  14.7 1.9 %collective-permute-start.1 = (f32[1,1024]{1,0:T(1,128)S(1)}, f32[1,1024]{1,0:T(1,128)S(1)}, u32[]{:S(2)}, u32[]{:S(2)}) collective-permute-start(f32[1,1024]{1,0:T(1,128)S(1)} %get-tuple-element.33), channel_id=1, source_target_pairs={{128,0},{256,128},{384,256},{512,384},{640,512},{768,640},{896,768... | collective-permute-start | bytes 12296 | tf_op jit(solution)/shard_map/ppermute | solution.py:22
  16.7 0.1 copy.179
  16.8 0.1 reshape.255
  17.0 13.2 %gather_fusion.1 = f32[2000]{0:T(1024)S(1)} fusion(f32[512]{0:T(512)S(1)} %multiply_add_fusion.3, s32[2048]{0:T(1024)S(1)} %pad_clamp_fusion.1), kind=kCustom, calls=%fused_computation.1 | custom fusion | bytes 24000 | tf_op jit(solution)/shard_map/gather | solution.py:104
  30.2 0.1 reshape.172
  30.3 0.2 fusion.48
  30.5 0.2 fusion.26
  30.7 0.2 convolution_bitcast_fusion.2
  31.0 0.1 copy.157
  31.2 10.9 %gather_fusion = f32[4000,3]{1,0:T(8,128)S(1)} fusion(f32[3,1024]{0,1:T(8,128)S(1)} %copy.159, s32[4096]{0:T(1024)S(1)} %pad_clamp_fusion), kind=kCustom, calls=%fused_computation | custom fusion | bytes 112000 | tf_op jit(solution)/shard_map/gather | solution.py:81
  42.1 0.9 copy.160
  43.1 0.4 fusion.47
  43.5 0.4 fusion.13
  43.9 0.4 convolution_bitcast_fusion.1
  44.4 0.1 copy.184
  44.6 0.1 multiply_divide_fusion
  44.8 0.3 fusion.22
  45.1 0.3 fusion.24
  45.6 0.1 copy.158
  45.8 0.1 copy.166
  46.0 0.1 maximum_multiply_fusion
  46.2 0.1 broadcast_divide_fusion
  46.3 0.2 fusion.7
  46.6 0.5 fusion.11
  47.0 0.5 fusion.9
  47.5 0.3 fusion.4
  47.8 0.5 fusion.2
  48.4 0.1 reshape.257
  48.5 14.6 %scatter_custom_fusion.1 = f32[512]{0:T(512)S(1)} fusion(s32[2000]{0:T(1024)S(1)} %reshape.255, f32[2000]{0:T(1024)S(1)} %reshape.257, f32[]{:T(128)} %constant.9.clone.1), kind=kCustom, calls=%fused_computation.113 | custom fusion | flops 2000 | bytes 2052 | tf_op jit(solution)/shard_map/scatter-add | solution.py:116
  63.2 14.7 %scatter_fusion = f32[512]{0:T(512)S(1)} fusion(f32[512]{0:T(512)S(1)} %scatter_custom_fusion.1, s32[2048]{0:T(1024)S(1)} %bitcast.173, f32[2048]{0:T(1024)S(1)} %bitcast.174), kind=kCustom, calls=%fused_computation.10 | custom fusion | flops 2048 | bytes 32768 | tf_op jit(solution)/shard_map/scatter-add | solution.py:162
  77.9 0.8 gather_fusion.3
  78.7 1.9 %collective-permute-start.2 = (f32[1,48]{1,0:T(1,128)S(1)}, f32[1,48]{1,0:T(1,128)S(1)}, u32[]{:S(2)}, u32[]{:S(2)}) collective-permute-start(f32[1,48]{1,0:T(1,128)S(1)} %bitcast.179), channel_id=1, source_target_pairs={{0,1},{1,2},{2,3},{3,4},{4,5},{5,6},{6,7},{7,8},{8,9},{9,10},{10,1... | collective-permute-start | bytes 584 | tf_op jit(solution)/shard_map/ppermute | solution.py:20
  80.6 0.8 gather_fusion.4
  81.4 18.0 %collective-permute-start.3 = (f32[1,48]{1,0:T(1,128)S(1)}, f32[1,48]{1,0:T(1,128)S(1)}, u32[]{:S(2)}, u32[]{:S(2)}) collective-permute-start(f32[1,48]{1,0:T(1,128)S(1)} %bitcast.178), channel_id=1, source_target_pairs={{1,0},{2,1},{3,2},{4,3},{5,4},{6,5},{7,6},{8,7},{9,8},{10,9},{11,1... | collective-permute-start | bytes 584 | tf_op jit(solution)/shard_map/ppermute | solution.py:22
  99.3 0.9 scatter_fusion.1
  100.2 0.4 collective-permute-done.3
  100.6 0.9 scatter_fusion.2
  101.5 0.6 multiply_add_fusion.2
  102.1 13.2 %gather_fusion.5 = f32[2048]{0:T(1024)S(1)} fusion(f32[512]{0:T(512)S(1)} %get-tuple-element.21, s32[2048]{0:T(1024)S(1)} %bitcast_clamp_fusion), kind=kCustom, calls=%fused_computation.5 | custom fusion | bytes 24576 | tf_op jit(solution)/shard_map/gather | solution.py:171
  115.4 7.9 %collective-permute-start.4 = (f32[1,1024]{1,0:T(1,128)S(1)}, f32[1,1024]{1,0:T(1,128)S(1)}, u32[]{:S(2)}, u32[]{:S(2)}) collective-permute-start(f32[1,1024]{1,0:T(1,128)S(1)} %get-tuple-element.28), channel_id=1, source_target_pairs={{0,128},{128,256},{256,384},{384,512},{512,640},{640,768},{768,896... | collective-permute-start | bytes 12296 | tf_op jit(solution)/shard_map/ppermute | solution.py:20
  123.2 2.1 %collective-permute-start.5 = (f32[1,1024]{1,0:T(1,128)S(1)}, f32[1,1024]{1,0:T(1,128)S(1)}, u32[]{:S(2)}, u32[]{:S(2)}) collective-permute-start(f32[1,1024]{1,0:T(1,128)S(1)} %get-tuple-element.29), channel_id=1, source_target_pairs={{128,0},{256,128},{384,256},{512,384},{640,512},{768,640},{896,768... | collective-permute-start | bytes 12296 | tf_op jit(solution)/shard_map/ppermute | solution.py:22
  125.5 0.8 copy.212
  126.3 22.8 %scatter_custom_fusion = f32[3,1024]{0,1:T(8,128)S(1)} fusion(s32[4000]{0:T(1024)S(1)} %reshape.247, f32[4000,3]{1,0:T(8,128)S(1)} %bitcast.164, f32[]{:T(128)} %constant.9.clone.1), kind=kCustom, calls=%fused_computation.47 | custom fusion | flops 12000 | bytes 12292 | tf_op jit(solution)/shard_map/scatter-add | solution.py:95
  149.2 0.4 copy.216
  149.6 11.6 %scatter_custom_fusion.5 = f32[3,1024]{0,1:T(8,128)S(1)} fusion(s32[2048]{0:T(1024)S(1)} %bitcast.175, f32[2048,3]{1,0:T(8,128)S(1)} %bitcast.168, f32[]{:T(128)} %constant.9.clone.1), kind=kCustom, calls=%fused_computation.45 | custom fusion | flops 6144 | bytes 12292 | tf_op jit(solution)/shard_map/scatter-add | solution.py:178
  161.2 0.6 gather_fusion.6
  161.9 1.9 %collective-permute-start.6 = (f32[1,3,96]{1,2,0:T(8,128)S(1)}, f32[1,3,96]{1,2,0:T(8,128)S(1)}, u32[]{:S(2)}, u32[]{:S(2)}) collective-permute-start(f32[1,3,96]{1,2,0:T(8,128)S(1)} %bitcast.181), channel_id=1, source_target_pairs={{0,1},{1,2},{2,3},{3,4},{4,5},{5,6},{6,7},{7,8},{8,9},{9,10},{10,1... | collective-permute-start | bytes 3464 | tf_op jit(solution)/shard_map/ppermute | solution.py:20
  163.8 0.6 gather_fusion.7
  164.4 5.7 %collective-permute-start.7 = (f32[1,3,96]{1,2,0:T(8,128)S(1)}, f32[1,3,96]{1,2,0:T(8,128)S(1)}, u32[]{:S(2)}, u32[]{:S(2)}) collective-permute-start(f32[1,3,96]{1,2,0:T(8,128)S(1)} %bitcast.180), channel_id=1, source_target_pairs={{1,0},{2,1},{3,2},{4,3},{5,4},{6,5},{7,6},{8,7},{9,8},{10,9},{11,1... | collective-permute-start | bytes 3464 | tf_op jit(solution)/shard_map/ppermute | solution.py:22
  170.2 0.2 copy.197
  170.4 0.2 copy.198
  170.7 1.3 scatter_custom_fusion.6
  172.0 1.3 scatter_custom_fusion.7
  173.3 0.2 multiply_add_fusion
  173.5 0.8 copy.199
  174.3 0.8 copy.200
  (97 shorter events, 1.1 us)
Async XLA Ops:
  0.6 16.0 %copy-start.12 = (s32[125,16]{0,1:T(8,128)S(1)}, s32[125,16]{0,1:T(8,128)}, u32[]{:S(2)}) copy-start(s32[125,16]{0,1:T(8,128)} %param.34) | copy-start | bytes 24004
  0.6 16.3 %copy-start.17 = (f32[512]{0:T(512)S(1)}, f32[512]{0:T(512)}, u32[]{:S(2)}) copy-start(f32[512]{0:T(512)} %param.30) | copy-start | bytes 6148
  0.7 16.3 %copy-start.13 = (f32[512]{0:T(512)S(1)}, f32[512]{0:T(512)}, u32[]{:S(2)}) copy-start(f32[512]{0:T(512)} %param.31) | copy-start | bytes 6148
  0.7 16.3 %copy-start.14 = (f32[512]{0:T(512)S(1)}, f32[512]{0:T(512)}, u32[]{:S(2)}) copy-start(f32[512]{0:T(512)} %param.32) | copy-start | bytes 6148
  9.7 53.4 %collective-permute-start = (f32[1,1024]{1,0:T(1,128)S(1)}, f32[1,1024]{1,0:T(1,128)S(1)}, u32[]{:S(2)}, u32[]{:S(2)}) collective-permute-start(f32[1,1024]{1,0:T(1,128)S(1)} %get-tuple-element.32), channel_id=1, source_target_pairs={{0,128},{128,256},{256,384},{384,512},{512,640},{640,768},{768,896... | collective-permute-start | bytes 12296 | tf_op jit(solution)/shard_map/ppermute | solution.py:20
  14.7 48.4 %collective-permute-start.1 = (f32[1,1024]{1,0:T(1,128)S(1)}, f32[1,1024]{1,0:T(1,128)S(1)}, u32[]{:S(2)}, u32[]{:S(2)}) collective-permute-start(f32[1,1024]{1,0:T(1,128)S(1)} %get-tuple-element.33), channel_id=1, source_target_pairs={{128,0},{256,128},{384,256},{512,384},{640,512},{768,640},{896,768... | collective-permute-start | bytes 12296 | tf_op jit(solution)/shard_map/ppermute | solution.py:22
  16.9 13.3 %copy-start.2 = (f32[5,5,1,1]{1,0,3,2:T(8,128)S(1)}, f32[5,5,1,1]{1,0,3,2:T(8,128)}, u32[]{:S(2)}) copy-start(f32[5,5,1,1]{1,0,3,2:T(8,128)} %constant.51) | copy-start | bytes 304
  17.0 14.0 %copy-start.9 = (s32[125,32]{0,1:T(8,128)S(1)}, s32[125,32]{0,1:T(8,128)}, u32[]{:S(2)}) copy-start(s32[125,32]{0,1:T(8,128)} %param.26) | copy-start | bytes 48004
  31.2 11.9 %copy-start.1 = (f32[5,5,1,1,1]{1,0,4,3,2:T(8,128)S(1)}, f32[5,5,1,1,1]{1,0,4,3,2:T(8,128)}, u32[]{:S(2)}) copy-start(f32[5,5,1,1,1]{1,0,4,3,2:T(8,128)} %constant.24) | copy-start | bytes 304
  42.1 2.3 %copy-start.16 = (bf16[125,16]{0,1:T(8,128)(2,1)S(1)}, bf16[125,16]{0,1:T(8,128)(2,1)}, u32[]{:S(2)}) copy-start(bf16[125,16]{0,1:T(8,128)(2,1)} %param.35) | copy-start | bytes 12004
  43.0 1.6 copy-start.21
  43.0 1.6 copy-start.7
  43.5 1.9 %copy-start.6 = (s32[2,1024]{1,0:T(2,128)S(1)}, s32[2,1024]{1,0:T(2,128)}, u32[]{:S(2)}) copy-start(s32[2,1024]{1,0:T(2,128)} %param.40) | copy-start | bytes 24580
  43.5 2.0 %copy-start.19 = (s32[2,48]{1,0:T(2,128)S(1)}, s32[2,48]{1,0:T(2,128)}, u32[]{:S(2)}) copy-start(s32[2,48]{1,0:T(2,128)} %param.38) | copy-start | bytes 1156
  44.3 1.3 copy-start.10
  44.4 1.4 copy-start.11
  44.6 1.4 copy-start.22
  45.5 0.7 copy-start.8
  46.3 1.2 copy-start.20
  77.8 23.6 %copy-start.18 = (f32[512]{0:T(512)S(1)}, f32[512]{0:T(512)}, u32[]{:S(2)}) copy-start(f32[512]{0:T(512)} %param.33) | copy-start | bytes 6148
  78.7 20.7 %collective-permute-start.2 = (f32[1,48]{1,0:T(1,128)S(1)}, f32[1,48]{1,0:T(1,128)S(1)}, u32[]{:S(2)}, u32[]{:S(2)}) collective-permute-start(f32[1,48]{1,0:T(1,128)S(1)} %bitcast.179), channel_id=1, source_target_pairs={{0,1},{1,2},{2,3},{3,4},{4,5},{5,6},{6,7},{7,8},{8,9},{9,10},{10,1... | collective-permute-start | bytes 584 | tf_op jit(solution)/shard_map/ppermute | solution.py:20
  81.4 19.2 %collective-permute-start.3 = (f32[1,48]{1,0:T(1,128)S(1)}, f32[1,48]{1,0:T(1,128)S(1)}, u32[]{:S(2)}, u32[]{:S(2)}) collective-permute-start(f32[1,48]{1,0:T(1,128)S(1)} %bitcast.178), channel_id=1, source_target_pairs={{1,0},{2,1},{3,2},{4,3},{5,4},{6,5},{7,6},{8,7},{9,8},{10,9},{11,1... | collective-permute-start | bytes 584 | tf_op jit(solution)/shard_map/ppermute | solution.py:22
  102.1 13.2 %copy-start = (f32[512]{0:T(512)}, f32[512]{0:T(512)S(1)}, u32[]{:S(2)}) copy-start(f32[512]{0:T(512)S(1)} %get-tuple-element.21) | copy-start | bytes 6148
  115.3 33.9 %copy-start.3 = (f32[3,2,1024]{2,1,0:T(2,128)S(1)}, f32[3,2,1024]{2,1,0:T(2,128)}, u32[]{:S(2)}) copy-start(f32[3,2,1024]{2,1,0:T(2,128)} %param.41) | copy-start | bytes 73732
  115.4 33.8 %collective-permute-start.4 = (f32[1,1024]{1,0:T(1,128)S(1)}, f32[1,1024]{1,0:T(1,128)S(1)}, u32[]{:S(2)}, u32[]{:S(2)}) collective-permute-start(f32[1,1024]{1,0:T(1,128)S(1)} %get-tuple-element.28), channel_id=1, source_target_pairs={{0,128},{128,256},{256,384},{384,512},{512,640},{640,768},{768,896... | collective-permute-start | bytes 12296 | tf_op jit(solution)/shard_map/ppermute | solution.py:20
  123.2 25.9 %collective-permute-start.5 = (f32[1,1024]{1,0:T(1,128)S(1)}, f32[1,1024]{1,0:T(1,128)S(1)}, u32[]{:S(2)}, u32[]{:S(2)}) collective-permute-start(f32[1,1024]{1,0:T(1,128)S(1)} %get-tuple-element.29), channel_id=1, source_target_pairs={{128,0},{256,128},{384,256},{512,384},{640,512},{768,640},{896,768... | collective-permute-start | bytes 12296 | tf_op jit(solution)/shard_map/ppermute | solution.py:22
  126.3 43.9 %copy-start.4 = (f32[3,1024]{1,0:T(4,128)S(1)}, f32[3,1024]{1,0:T(4,128)}, u32[]{:S(2)}) copy-start(f32[3,1024]{1,0:T(4,128)} %param.24) | copy-start | bytes 36868
  149.1 21.3 %copy-start.5 = (f32[3,1024]{1,0:T(4,128)S(1)}, f32[3,1024]{1,0:T(4,128)}, u32[]{:S(2)}) copy-start(f32[3,1024]{1,0:T(4,128)} %param.23) | copy-start | bytes 36868
  161.2 12.1 %copy-start.15 = (f32[1024]{0:T(1024)S(1)}, f32[1024]{0:T(1024)}, u32[]{:S(2)}) copy-start(f32[1024]{0:T(1024)} %param.25) | copy-start | bytes 12292
  161.9 8.8 %collective-permute-start.6 = (f32[1,3,96]{1,2,0:T(8,128)S(1)}, f32[1,3,96]{1,2,0:T(8,128)S(1)}, u32[]{:S(2)}, u32[]{:S(2)}) collective-permute-start(f32[1,3,96]{1,2,0:T(8,128)S(1)} %bitcast.181), channel_id=1, source_target_pairs={{0,1},{1,2},{2,3},{3,4},{4,5},{5,6},{6,7},{7,8},{8,9},{9,10},{10,1... | collective-permute-start | bytes 3464 | tf_op jit(solution)/shard_map/ppermute | solution.py:20
  164.4 7.5 %collective-permute-start.7 = (f32[1,3,96]{1,2,0:T(8,128)S(1)}, f32[1,3,96]{1,2,0:T(8,128)S(1)}, u32[]{:S(2)}, u32[]{:S(2)}) collective-permute-start(f32[1,3,96]{1,2,0:T(8,128)S(1)} %bitcast.180), channel_id=1, source_target_pairs={{1,0},{2,1},{3,2},{4,3},{5,4},{6,5},{7,6},{8,7},{9,8},{10,9},{11,1... | collective-permute-start | bytes 3464 | tf_op jit(solution)/shard_map/ppermute | solution.py:22
where the time goes:
time: 178 us; the launch traced here: 175 us
  other arithmetic  72.6 us (41%)
  local copies, waits for them, and re-layouts  51.8 us (29%)
  starting transfers between devices  44.4 us (25%)
  matrix products  4.19 us (2%)
    ppermute x4, starting transfers between devices, extended(): lax.ppermute(head, axis, [((i + 1) % count, i) for i in range(ends)])  27.7 us
    scatter-add x1, other arithmetic, solid_element_forces(): return jnp.zeros((3, node_count), jnp.float32).at[:, connectivity].add(el...  22.8 us
    ppermute x4, starting transfers between devices, extended(): lax.ppermute(tail, axis, [(i, (i + 1) % count) for i in range(ends)])  16.7 us
    scatter-add x1, other arithmetic, on_device(): fluid_force = fluid_force.at[fluid_target].add(arrived_motion, mode='drop')  14.7 us
    scatter-add x1, other arithmetic, fluid_element_forces(): return jnp.zeros((node_count,), jnp.float32).at[connectivity].add(element...  14.6 us
    gather x2, local copies, waits for them, and re-layouts, on_device(): potential_ddot_new[jnp.where(fluid_live, fluid_interface, 0)]  13.2 us
    gather x1, local copies, waits for them, and re-layouts, fluid_element_forces(): potential_values[connectivity].reshape(5, 5, 5, element_count)  13.2 us
    gather x2, local copies, waits for them, and re-layouts, solid_element_forces(): local_values = displaced[:, connectivity].reshape(3, 5, 5, 5, element_count)  11.8 us
  transfers between devices with their start and end apart: 8, of which 1 were waited for; matrix products, arithmetic and copies ran while one was open for 42% of the time, Pallas kernels for 0%

commit v1 on v0

v1 whole, which is shorter than its diff:
```python
import math

import jax
import jax.numpy as jnp
import numpy as np
from jax import lax
from jax.experimental import pallas as pl
from jax.experimental.pallas import tpu as pltpu
from jax.sharding import PartitionSpec as P

time_step = 0.4
MESH = pl.DeviceIdType.MESH
LANES = 128
f32 = jnp.float32
bf16 = jnp.bfloat16


def gll_tables():
    points = np.array([-1.0, -math.sqrt(3.0 / 7.0), 0.0, math.sqrt(3.0 / 7.0), 1.0])
    weights = np.array([0.1, 49.0 / 90.0, 32.0 / 45.0, 49.0 / 90.0, 0.1])
    products = np.array(
        [np.prod([points[i] - points[j] for j in range(5) if j != i]) for i in range(5)]
    )
    derivative = np.zeros((5, 5))
    for i in range(5):
        for j in range(5):
            if i != j:
                derivative[i, j] = products[i] / (products[j] * (points[i] - points[j]))
            else:
                derivative[i, j] = sum(1.0 / (points[i] - points[k]) for k in range(5) if k != i)
    weight_cube = weights[:, None, None] * weights[None, :, None] * weights[None, None, :]
    return derivative.astype(np.float32), weight_cube.astype(np.float32)


def derivative_matrices():
    derivative, weight_cube = gll_tables()
    eye = np.eye(5, dtype=np.float32)
    whole = np.zeros((3, LANES, LANES), np.float32)
    whole[0, :125, :125] = np.kron(derivative, np.kron(eye, eye))
    whole[1, :125, :125] = np.kron(eye, np.kron(derivative, eye))
    whole[2, :125, :125] = np.kron(eye, np.kron(eye, derivative))
    whole = whole.reshape(3 * LANES, LANES)
    high = whole.astype(jnp.bfloat16)
    low = (whole - high.astype(np.float32)).astype(jnp.bfloat16)
    weights = np.zeros((8, LANES), np.float32)
    weights[:, :125] = weight_cube.reshape(1, 125)
    return high, low, weights


def split(x):
    high = x.astype(bf16)
    return high, (x - high.astype(f32)).astype(bf16)


def dot(a, b, dims):
    return lax.dot_general(a, b, (dims, ((), ())), preferred_element_type=f32)


def dot_split(x, high, low, dims):
    x_high, x_low = split(x)
    return dot(x_high, high, dims) + dot(x_low, high, dims) + dot(x_high, low, dims)


def lookup(tables, hi, lo):
    out = [jnp.zeros(hi.shape, f32) for _ in tables]
    for h in range(len(tables[0])):
        here = hi == h
        for c, rows in enumerate(tables):
            picked = jnp.take_along_axis(
                jnp.broadcast_to(rows[h], hi.shape), lo, axis=1, mode="promise_in_bounds"
            )
            out[c] = jnp.where(here, picked, out[c])
    return out


def mark_low(marks_ref, lo):
    sublane = lax.broadcasted_iota(jnp.int32, (LANES, LANES), 0)
    for row in range(lo.shape[0]):
        line = jnp.broadcast_to(lo[row : row + 1], (LANES, LANES))
        marks_ref[:, row * LANES : (row + 1) * LANES] = jnp.where(line == sublane, 1.0, 0.0).astype(
            bf16
        )


def spread_high(terms_ref, hi, values):
    sublane = lax.broadcasted_iota(jnp.int32, (8, LANES), 0)
    parts = []
    for value in values:
        high = value.astype(bf16).astype(f32)
        parts.append((high, value - high))
    for row in range(hi.shape[0]):
        here = jnp.broadcast_to(hi[row : row + 1], (8, LANES)) == sublane
        for c, pair in enumerate(parts):
            both = [
                jnp.where(here, jnp.broadcast_to(part[row : row + 1], (8, LANES)), 0.0)
                for part in pair
            ]
            terms_ref[16 * c : 16 * c + 16, row * LANES : (row + 1) * LANES] = jnp.concatenate(
                both, axis=0
            ).astype(bf16)


def collect(terms_ref, marks_ref):
    sums = dot(terms_ref[...], marks_ref[...], ((1,), (1,)))
    return [
        sums[16 * c : 16 * c + 8] + sums[16 * c + 8 : 16 * c + 16]
        for c in range(terms_ref.shape[0] // 16)
    ]


def rows_of(ref, lead):
    line = ref[lead]
    return jnp.concatenate([line[:, LANES * t : LANES * (t + 1)] for t in range(8)], axis=0)


def both_sides(ref, *lead):
    return jnp.concatenate(
        [rows_of(ref, (*lead, slice(p, p + 1), slice(None))) for p in range(2)], axis=0
    )


def step_kernel(n_region, n_dom, n_inputs, *refs):
    sources = refs[:n_inputs]
    velocity_out, acceleration_out, dot_out, ddot_out = refs[n_inputs : n_inputs + 4]
    held = refs[n_inputs + 4 : 2 * n_inputs + 4]
    (
        load_sem,
        send_sem,
        recv_sem,
        motion_send,
        motion_recv,
        pressure_send,
        pressure_recv,
        fluid_send,
        fluid_recv,
        solid_send,
        solid_recv,
        index_pad,
        field_pad,
        fluid_index_pad,
        fluid_field_pad,
        element_terms,
        element_marks,
        fluid_terms,
        fluid_marks,
        slot_terms,
        slot_marks,
        arrived_terms,
        arrived_marks,
    ) = refs[2 * n_inputs + 4 :]
    (
        displacement,
        velocity,
        acceleration,
        solid_interface,
        interface_normal,
        potential,
        potential_dot,
        potential_ddot,
        fluid_connectivity,
        density_inverse,
        fluid_inverse_size,
        matrix_high,
        matrix_low,
        weight_cube,
        fluid_interface,
        fluid_halo,
        fluid_mass_inverse,
        connectivity,
        lame_lambda,
        shear_modulus,
        inverse_size,
        solid_halo,
        solid_mass_inverse,
    ) = held

    region, dom = lax.axis_index("region"), lax.axis_index("dom")
    above = (lax.rem(region + 1, n_region), dom)
    below = (lax.rem(region + n_region - 1, n_region), dom)
    upper = (region, lax.rem(dom + 1, n_dom))
    lower = (region, lax.rem(dom + n_dom - 1, n_dom))

    barrier = pltpu.get_barrier_semaphore()
    for other in (above, below, upper, lower):
        pl.semaphore_signal(barrier, inc=1, device_id=other, device_id_type=MESH)
    loads = [
        pltpu.make_async_copy(source, target, load_sem.at[i])
        for i, (source, target) in enumerate(zip(sources, held))
    ]
    for load in loads:
        load.start()

    def send(send_ref, recv_ref, flow, to_higher, to_lower):
        copies = []
        for side, target in ((0, to_higher), (1, to_lower)):
            copy = pltpu.make_async_remote_copy(
                src_ref=send_ref.at[side],
                dst_ref=recv_ref.at[side],
                send_sem=send_sem.at[2 * flow + side],
                recv_sem=recv_sem.at[2 * flow + side],
                device_id=target,
                device_id_type=MESH,
            )
            copy.start()
            copies.append(copy)
        return copies

    for i in range(5):
        loads[i].wait()
    half_square = 0.5 * time_step * time_step
    predicted = displacement[...] + time_step * velocity[...] + half_square * acceleration[...]
    solid_tables = [
        [predicted[c : c + 1, LANES * h : LANES * (h + 1)] for h in range(8)] for c in range(3)
    ]
    slots = both_sides(solid_interface)
    slot_hi, slot_lo = slots >> 7, slots & 127
    normals = [both_sides(interface_normal, c) for c in range(3)]
    moved = lookup(solid_tables, slot_hi, slot_lo)
    motion = normals[0] * moved[0] + normals[1] * moved[1] + normals[2] * moved[2]
    motion_send[0] = motion[8:]
    motion_send[1] = motion[:8]
    pl.semaphore_wait(barrier, 4)
    motion_copies = send(motion_send, motion_recv, 0, above, below)

    for i in range(5, 14):
        loads[i].wait()
    fluid_predicted = (
        potential[...] + time_step * potential_dot[...] + half_square * potential_ddot[...]
    )
    fluid_table = [[fluid_predicted[h : h + 1] for h in range(4)]]
    fluid_index_pad[...] = jnp.full(fluid_index_pad.shape, -1, jnp.int32)
    fluid_index_pad[:, :125] = fluid_connectivity[...]
    fluid_field_pad[...] = jnp.zeros(fluid_field_pad.shape, f32)
    fluid_field_pad[:, :125] = density_inverse[...].astype(f32)
    fluid_index = fluid_index_pad[...]
    fluid_hi, fluid_lo = fluid_index >> 7, fluid_index & 127
    local = lookup(fluid_table, fluid_hi, fluid_lo)[0]
    high, low = matrix_high[...], matrix_low[...]
    gradient = dot_split(local, high, low, ((1,), (1,)))

    def column(line, count):
        rows = lax.broadcasted_iota(jnp.int32, (count, count), 0)
        columns = lax.broadcasted_iota(jnp.int32, (count, count), 1)
        wide = jnp.broadcast_to(line, (count, count))
        return jnp.sum(jnp.where(rows == columns, wide, 0.0), axis=1, keepdims=True)

    weights = weight_cube[0:1]
    fluid_factor = weights * fluid_field_pad[...] * (-1.0 / column(fluid_inverse_size[...], 16))
    weighted = jnp.concatenate(
        [gradient[:, LANES * b : LANES * (b + 1)] * fluid_factor for b in range(3)], axis=1
    )
    element = dot_split(weighted, high, low, ((1,), (0,)))
    mark_low(fluid_marks, fluid_lo)
    spread_high(fluid_terms, fluid_hi, [element])
    fluid_force = collect(fluid_terms, fluid_marks)[0]

    for i in range(14, 17):
        loads[i].wait()
    fluid_slots = both_sides(fluid_interface)
    arrived_hi, arrived_lo = fluid_slots >> 7, fluid_slots & 127
    mark_low(arrived_marks, arrived_lo)
    rim = fluid_halo[...]
    rim_hi, rim_lo = rim >> 7, rim & 127
    lane8 = lax.broadcasted_iota(jnp.int32, (8, LANES), 0) * LANES + lax.broadcasted_iota(
        jnp.int32, (8, LANES), 1
    )
    for copy in motion_copies:
        copy.wait_recv()
    spread_high(
        arrived_terms, arrived_hi, [jnp.concatenate([motion_recv[0], motion_recv[1]], axis=0)]
    )
    fluid_total = fluid_force + collect(arrived_terms, arrived_marks)[0]

    def halo_tables(halo_ref, count):
        found = []
        nodes = halo_ref[...]
        for side in range(2):
            found.append(nodes[side : side + 1])
        return found

    def rim_index(halo_ref, pad_ref, count):
        pad_ref[...] = jnp.full(pad_ref.shape, -1, jnp.int32)
        pad_ref[0:2, :count] = halo_ref[...]
        return pad_ref[...]

    fluid_rim = rim_index(fluid_halo, index_pad.at[0:8], 48)
    rim_values = lookup(
        [[fluid_total[h : h + 1] for h in range(4)]], fluid_rim >> 7, fluid_rim & 127
    )[0]
    fluid_send[0] = rim_values[1:2]
    fluid_send[1] = rim_values[0:1]
    fluid_copies = send(fluid_send, fluid_recv, 1, upper, lower)

    def slot_of_node(rim):
        out = []
        marks_lane = lax.broadcasted_iota(jnp.int32, (LANES, LANES), 0)
        sublane = lax.broadcasted_iota(jnp.int32, (8, LANES), 0)
        number = lax.broadcasted_iota(jnp.int32, (8, LANES), 1).astype(f32) + 1.0
        for side in range(2):
            line = rim[side : side + 1]
            marks = jnp.where(
                jnp.broadcast_to(line & 127, (LANES, LANES)) == marks_lane, 1.0, 0.0
            ).astype(bf16)
            terms = jnp.where(jnp.broadcast_to(line >> 7, (8, LANES)) == sublane, number, 0.0)
            out.append(dot(terms.astype(bf16), marks, ((1,), (1,))).astype(jnp.int32) - 1)
        return out

    def add_rims(total, arrived, places):
        for line, place in zip(arrived, places):
            picked = jnp.take_along_axis(
                jnp.broadcast_to(line, place.shape),
                jnp.maximum(place, 0),
                axis=1,
                mode="promise_in_bounds",
            )
            total = total + jnp.where(place >= 0, picked, 0.0)
        return total

    fluid_places = slot_of_node(fluid_rim)

    for i in range(17, 23):
        loads[i].wait()
    index_pad[...] = jnp.full(index_pad.shape, -1, jnp.int32)
    index_pad[:, :125] = connectivity[...]
    index = index_pad[...]
    hi, lo = index >> 7, index & 127
    values = lookup(solid_tables, hi, lo)
    gradient = dot_split(jnp.concatenate(values, axis=0), high, low, ((1,), (1,)))
    field_pad[...] = jnp.zeros(field_pad.shape, f32)
    field_pad[:, :125] = lame_lambda[...].astype(f32)
    lame = field_pad[...]
    field_pad[:, :125] = shear_modulus[...].astype(f32)
    shear = field_pad[...]
    factor = weights * (-1.0 / column(inverse_size[...], 32))
    lame, shear = lame * factor, shear * factor
    grad = [
        [gradient[32 * c : 32 * c + 32, LANES * b : LANES * (b + 1)] for b in range(3)]
        for c in range(3)
    ]
    trace = lame * (grad[0][0] + grad[1][1] + grad[2][2])
    stress = [[None] * 3 for _ in range(3)]
    for a in range(3):
        stress[a][a] = trace + shear * (grad[a][a] + grad[a][a])
        for b in range(a):
            stress[a][b] = stress[b][a] = shear * (grad[a][b] + grad[b][a])
    weighted = jnp.concatenate([jnp.concatenate(row, axis=1) for row in stress], axis=0)
    element = dot_split(weighted, high, low, ((1,), (0,)))
    mark_low(element_marks, lo)
    spread_high(element_terms, hi, [element[32 * c : 32 * c + 32] for c in range(3)])

    for copy in fluid_copies:
        copy.wait_recv()
    assembled = add_rims(fluid_total, [fluid_recv[0], fluid_recv[1]], fluid_places)
    ddot = fluid_mass_inverse[...] * assembled[:4]
    pressure = lookup([[ddot[h : h + 1] for h in range(4)]], arrived_hi, arrived_lo)[0]
    pressure_send[0] = pressure[8:]
    pressure_send[1] = pressure[:8]
    pressure_copies = send(pressure_send, pressure_recv, 2, above, below)
    ddot_out[...] = ddot
    dot_out[...] = potential_dot[...] + 0.5 * time_step * (potential_ddot[...] + ddot)

    force = collect(element_terms, element_marks)
    mark_low(slot_marks, slot_lo)
    solid_rim = rim_index(solid_halo, index_pad.at[0:8], 96)
    solid_places = slot_of_node(solid_rim)
    for copy in pressure_copies:
        copy.wait_recv()
    arrived = jnp.concatenate([pressure_recv[0], pressure_recv[1]], axis=0)
    spread_high(slot_terms, slot_hi, [-(normal * arrived) for normal in normals])
    coupling = collect(slot_terms, slot_marks)
    total = [a + b for a, b in zip(force, coupling)]
    rim_values = lookup(
        [[t[h : h + 1] for h in range(8)] for t in total], solid_rim >> 7, solid_rim & 127
    )
    for c in range(3):
        solid_send[0, c : c + 1] = rim_values[c][1:2]
        solid_send[1, c : c + 1] = rim_values[c][0:1]
    solid_copies = send(solid_send, solid_recv, 3, upper, lower)
    mass = solid_mass_inverse[...]
    base = [
        rows_of(velocity, (slice(c, c + 1), slice(None)))
        + 0.5 * time_step * rows_of(acceleration, (slice(c, c + 1), slice(None)))
        for c in range(3)
    ]
    for copy in solid_copies:
        copy.wait_recv()
    for c in range(3):
        arrived = [solid_recv[side, c : c + 1] for side in range(2)]
        new = mass * add_rims(total[c], arrived, solid_places)
        speed = base[c] + 0.5 * time_step * new
        for h in range(8):
            acceleration_out[c : c + 1, LANES * h : LANES * (h + 1)] = new[h : h + 1]
            velocity_out[c : c + 1, LANES * h : LANES * (h + 1)] = speed[h : h + 1]
    for copy in motion_copies + fluid_copies + pressure_copies + solid_copies:
        copy.wait_send()


def on_device(
    n_region,
    n_dom,
    displacement,
    velocity,
    acceleration,
    solid_mass_inverse,
    connectivity,
    lame_lambda,
    shear_modulus,
    inverse_size,
    potential,
    potential_dot,
    potential_ddot,
    fluid_mass_inverse,
    fluid_connectivity,
    density_inverse,
    fluid_inverse_size,
    solid_halo,
    fluid_halo,
    solid_interface,
    fluid_interface,
    interface_normal,
):
    high, low, weights = derivative_matrices()
    operands = (
        displacement,
        velocity,
        acceleration,
        solid_interface,
        interface_normal,
        potential.reshape(4, LANES),
        potential_dot.reshape(4, LANES),
        potential_ddot.reshape(4, LANES),
        fluid_connectivity.T,
        density_inverse.T,
        fluid_inverse_size.reshape(1, 16),
        jnp.asarray(high),
        jnp.asarray(low),
        jnp.asarray(weights),
        fluid_interface,
        fluid_halo,
        fluid_mass_inverse.reshape(4, LANES),
        connectivity.T,
        lame_lambda.T,
        shear_modulus.T,
        inverse_size.reshape(1, 32),
        solid_halo,
        solid_mass_inverse.reshape(8, LANES),
    )
    count = len(operands)
    vmem = pltpu.VMEM
    outs = pl.pallas_call(
        lambda *refs: step_kernel(n_region, n_dom, count, *refs),
        out_shape=(
            jax.ShapeDtypeStruct((3, 1024), f32),
            jax.ShapeDtypeStruct((3, 1024), f32),
            jax.ShapeDtypeStruct((4, LANES), f32),
            jax.ShapeDtypeStruct((4, LANES), f32),
        ),
        in_specs=[pl.BlockSpec(memory_space=pl.ANY)] * count,
        out_specs=[pl.BlockSpec(memory_space=vmem)] * 4,
        scratch_shapes=[vmem(x.shape, x.dtype) for x in operands]
        + [
            pltpu.SemaphoreType.DMA((count,)),
            pltpu.SemaphoreType.DMA((8,)),
            pltpu.SemaphoreType.DMA((8,)),
            vmem((2, 8, LANES), f32),
            vmem((2, 8, LANES), f32),
            vmem((2, 8, LANES), f32),
            vmem((2, 8, LANES), f32),
            vmem((2, 1, LANES), f32),
            vmem((2, 1, LANES), f32),
            vmem((2, 3, LANES), f32),
            vmem((2, 3, LANES), f32),
            vmem((32, LANES), jnp.int32),
            vmem((32, LANES), f32),
            vmem((16, LANES), jnp.int32),
            vmem((16, LANES), f32),
            vmem((48, 32 * LANES), bf16),
            vmem((LANES, 32 * LANES), bf16),
            vmem((16, 16 * LANES), bf16),
            vmem((LANES, 16 * LANES), bf16),
            vmem((48, 16 * LANES), bf16),
            vmem((LANES, 16 * LANES), bf16),
            vmem((16, 16 * LANES), bf16),
            vmem((LANES, 16 * LANES), bf16),
        ],
        compiler_params=pltpu.CompilerParams(collective_id=0, has_side_effects=True),
        name="newmark_step",
    )(*operands)
    return outs[0], outs[1], outs[2].reshape(512), outs[3].reshape(512)


def solution(mesh):
    cut = ("region", "dom")
    line, plane = P(cut), P(None, cut)
    in_specs = (
        (plane,) * 3
        + (line,)
        + (plane,) * 3
        + (line,) * 5
        + (plane,) * 2
        + (line,)
        + (plane,) * 4
        + (P(None, None, cut),)
    )
    n_region, n_dom = mesh.shape["region"], mesh.shape["dom"]
    return jax.shard_map(
        lambda *args: on_device(n_region, n_dom, *args),
        mesh=mesh,
        in_specs=in_specs,
        out_specs=(plane, plane, line, line),
        check_vma=False,
    )
```

time: 178 us -> 40.6 us (0.23)
  the two profiles are of different devices: /device:TPU:6 before, /device:TPU:1 now
where the time goes in v1:
time: 40.6 us; the launch traced here: 40.2 us
  Pallas kernels  36.3 us (89%)
  local copies, waits for them, and re-layouts  3.28 us (8%)
  between operations  0.66 us (2%)
    pallas_call x1, Pallas kernels, on_device(): pl.pallas_call(lambda *refs: step_kernel(n_region, n_dom, count, *refs),...  36.3 us
    unnamed x10, local copies, waits for them, and re-layouts  3.28 us

profile of v1, /device:TPU:1, one launch (start us, length us, event | category | flops | bytes accessed | tf_op | source)
XLA Modules:
  0.0 40.2 jit_solution(2216630603721817712)
XLA Ops:
  0.6 36.3 %newmark_step.1 = (f32[3,1024]{1,0:T(4,128)}, f32[3,1024]{1,0:T(4,128)}, f32[4,128]{1,0:T(4,128)}, f32[4,128]{1,0:T(4,128)}) custom-call(f32[3,1024]{1,0:T(4,128)} %refs_0_.1, f32[3,1024]{1,0:T(4,128)} %refs_1_.1, f32[3,1024]{1,0:T(4,128)} %refs_2_.1, s32[2,1024]{1,0:T(2,128)} %refs_3_.1, f32[3,2,1024]{2,1,0:T(2,128)} %refs_4_.1, f32[4,128]{1,0:T(4,128)} %bitcast.20, ...), custom_call_target="tpu_custom_call" | custom-call | tf_op jit(solution)/shard_map/newmark_step/pallas_call | solution.py:450
  36.9 0.0 copy-start
  37.0 1.3 %copy.31 = f32[3,1024]{1,0:T(4,128)} copy(f32[3,1024]{1,0:T(4,128)} %get-tuple-element.16) | data formatting | bytes 24576
  38.3 0.0 copy-done
  38.3 0.0 copy-start.2
  38.3 0.6 %copy.32 = f32[3,1024]{1,0:T(4,128)} copy(f32[3,1024]{1,0:T(4,128)S(1)} %copy-done) | data formatting | bytes 24576
  38.9 0.1 copy-done.2
  39.0 0.0 copy-start.1
  39.0 0.6 %copy.33 = f32[512]{0:T(512)} copy(f32[512]{0:T(512)S(1)} %bitcast.25) | data formatting | bytes 4096
  39.6 0.1 copy-done.1
  39.7 0.6 %copy.34 = f32[512]{0:T(512)} copy(f32[512]{0:T(512)S(1)} %bitcast.24) | data formatting | bytes 4096
Async XLA Ops:
  36.9 1.3 %copy-start = (f32[3,1024]{1,0:T(4,128)S(1)}, f32[3,1024]{1,0:T(4,128)}, u32[]{:S(2)}) copy-start(f32[3,1024]{1,0:T(4,128)} %get-tuple-element.17) | copy-start | bytes 36868
  38.3 0.7 %copy-start.2 = (f32[4,128]{1,0:T(4,128)S(1)}, f32[4,128]{1,0:T(4,128)}, u32[]{:S(2)}) copy-start(f32[4,128]{1,0:T(4,128)} %get-tuple-element.10) | copy-start | bytes 6148
  39.0 0.7 %copy-start.1 = (f32[4,128]{1,0:T(4,128)S(1)}, f32[4,128]{1,0:T(4,128)}, u32[]{:S(2)}) copy-start(f32[4,128]{1,0:T(4,128)} %get-tuple-element.11) | copy-start | bytes 6148

commit v2 on v1

--- a/solution.py
+++ b/solution.py
@@ -45,6 +45,13 @@
     weights = np.zeros((8, LANES), np.float32)
     weights[:, :125] = weight_cube.reshape(1, 125)
     return high, low, weights
+
+
+def when(condition, action):
+    if condition is None:
+        action()
+    else:
+        pl.when(condition)(action)
 
 
 def split(x):
@@ -180,9 +187,17 @@
     upper = (region, lax.rem(dom + 1, n_dom))
     lower = (region, lax.rem(dom + n_dom - 1, n_dom))
 
+    has_above, has_below = region < n_region - 1, region > 0
+    for ref in (motion_recv, pressure_recv):
+        ref[...] = jnp.zeros(ref.shape, f32)
     barrier = pltpu.get_barrier_semaphore()
-    for other in (above, below, upper, lower):
-        pl.semaphore_signal(barrier, inc=1, device_id=other, device_id_type=MESH)
+    for held_if, other in ((has_above, above), (has_below, below), (None, upper), (None, lower)):
+        when(
+            held_if,
+            lambda other=other: pl.semaphore_signal(
+                barrier, inc=1, device_id=other, device_id_type=MESH
+            ),
+        )
     loads = [
         pltpu.make_async_copy(source, target, load_sem.at[i])
         for i, (source, target) in enumerate(zip(sources, held))
@@ -190,7 +205,7 @@
     for load in loads:
         load.start()
 
-    def send(send_ref, recv_ref, flow, to_higher, to_lower):
+    def send(send_ref, recv_ref, flow, to_higher, to_lower, conditions=(None, None)):
         copies = []
         for side, target in ((0, to_higher), (1, to_lower)):
             copy = pltpu.make_async_remote_copy(
@@ -201,9 +216,15 @@
                 device_id=target,
                 device_id_type=MESH,
             )
-            copy.start()
-            copies.append(copy)
+            when(conditions[side], copy.start)
+            copies.append((copy, conditions[side], conditions[1 - side]))
         return copies
+
+    def receive(copies):
+        for copy, _, condition in copies:
+            when(condition, copy.wait_recv)
+
+    ends = (has_above, has_below)
 
     for i in range(5):
         loads[i].wait()
@@ -219,8 +240,10 @@
     motion = normals[0] * moved[0] + normals[1] * moved[1] + normals[2] * moved[2]
     motion_send[0] = motion[8:]
     motion_send[1] = motion[:8]
-    pl.semaphore_wait(barrier, 4)
-    motion_copies = send(motion_send, motion_recv, 0, above, below)
+    peers = 2 + lax.div(region + n_region - 1, n_region)
+    peers = peers + lax.div(2 * n_region - 2 - region, n_region)
+    pl.semaphore_wait(barrier, peers)
+    motion_copies = send(motion_send, motion_recv, 0, above, below, ends)
 
     for i in range(5, 14):
         loads[i].wait()
@@ -259,24 +282,11 @@
     fluid_slots = both_sides(fluid_interface)
     arrived_hi, arrived_lo = fluid_slots >> 7, fluid_slots & 127
     mark_low(arrived_marks, arrived_lo)
-    rim = fluid_halo[...]
-    rim_hi, rim_lo = rim >> 7, rim & 127
-    lane8 = lax.broadcasted_iota(jnp.int32, (8, LANES), 0) * LANES + lax.broadcasted_iota(
-        jnp.int32, (8, LANES), 1
-    )
-    for copy in motion_copies:
-        copy.wait_recv()
+    receive(motion_copies)
     spread_high(
         arrived_terms, arrived_hi, [jnp.concatenate([motion_recv[0], motion_recv[1]], axis=0)]
     )
     fluid_total = fluid_force + collect(arrived_terms, arrived_marks)[0]
-
-    def halo_tables(halo_ref, count):
-        found = []
-        nodes = halo_ref[...]
-        for side in range(2):
-            found.append(nodes[side : side + 1])
-        return found
 
     def rim_index(halo_ref, pad_ref, count):
         pad_ref[...] = jnp.full(pad_ref.shape, -1, jnp.int32)
@@ -348,14 +358,13 @@
     mark_low(element_marks, lo)
     spread_high(element_terms, hi, [element[32 * c : 32 * c + 32] for c in range(3)])
 
-    for copy in fluid_copies:
-        copy.wait_recv()
+    receive(fluid_copies)
     assembled = add_rims(fluid_total, [fluid_recv[0], fluid_recv[1]], fluid_places)
     ddot = fluid_mass_inverse[...] * assembled[:4]
     pressure = lookup([[ddot[h : h + 1] for h in range(4)]], arrived_hi, arrived_lo)[0]
     pressure_send[0] = pressure[8:]
     pressure_send[1] = pressure[:8]
-    pressure_copies = send(pressure_send, pressure_recv, 2, above, below)
+    pressure_copies = send(pressure_send, pressure_recv, 2, above, below, ends)
     ddot_out[...] = ddot
     dot_out[...] = potential_dot[...] + 0.5 * time_step * (potential_ddot[...] + ddot)
 
@@ -363,8 +372,7 @@
     mark_low(slot_marks, slot_lo)
     solid_rim = rim_index(solid_halo, index_pad.at[0:8], 96)
     solid_places = slot_of_node(solid_rim)
-    for copy in pressure_copies:
-        copy.wait_recv()
+    receive(pressure_copies)
     arrived = jnp.concatenate([pressure_recv[0], pressure_recv[1]], axis=0)
     spread_high(slot_terms, slot_hi, [-(normal * arrived) for normal in normals])
     coupling = collect(slot_terms, slot_marks)
@@ -382,8 +390,7 @@
         + 0.5 * time_step * rows_of(acceleration, (slice(c, c + 1), slice(None)))
         for c in range(3)
     ]
-    for copy in solid_copies:
-        copy.wait_recv()
+    receive(solid_copies)
     for c in range(3):
         arrived = [solid_recv[side, c : c + 1] for side in range(2)]
         new = mass * add_rims(total[c], arrived, solid_places)
@@ -391,8 +398,19 @@
         for h in range(8):
             acceleration_out[c : c + 1, LANES * h : LANES * (h + 1)] = new[h : h + 1]
             velocity_out[c : c + 1, LANES * h : LANES * (h + 1)] = speed[h : h + 1]
-    for copy in motion_copies + fluid_copies + pressure_copies + solid_copies:
-        copy.wait_send()
+    for copy, condition, _ in motion_copies + fluid_copies + pressure_copies + solid_copies:
+        when(condition, copy.wait_send)
+
+
+def write_kernel(*refs):
+    sem = refs[-1]
+    copies = [
+        pltpu.make_async_copy(refs[i], refs[4 + i], sem.at[i]) for i in range(4)
+    ]
+    for copy in copies:
+        copy.start()
+    for copy in copies:
+        copy.wait()
 
 
 def on_device(
@@ -447,14 +465,10 @@
     )
     count = len(operands)
     vmem = pltpu.VMEM
+    shapes = ((3, 1024), (3, 1024), (4, LANES), (4, LANES))
     outs = pl.pallas_call(
         lambda *refs: step_kernel(n_region, n_dom, count, *refs),
-        out_shape=(
-            jax.ShapeDtypeStruct((3, 1024), f32),
-            jax.ShapeDtypeStruct((3, 1024), f32),
-            jax.ShapeDtypeStruct((4, LANES), f32),
-            jax.ShapeDtypeStruct((4, LANES), f32),
-        ),
+        out_shape=tuple(pltpu.VMEM(shape, f32) for shape in shapes),
         in_specs=[pl.BlockSpec(memory_space=pl.ANY)] * count,
         out_specs=[pl.BlockSpec(memory_space=vmem)] * 4,
         scratch_shapes=[vmem(x.shape, x.dtype) for x in operands]
@@ -486,6 +500,14 @@
         compiler_params=pltpu.CompilerParams(collective_id=0, has_side_effects=True),
         name="newmark_step",
     )(*operands)
+    outs = pl.pallas_call(
+        write_kernel,
+        out_shape=tuple(jax.ShapeDtypeStruct(shape, f32) for shape in shapes),
+        in_specs=[pl.BlockSpec(memory_space=vmem)] * 4,
+        out_specs=[pl.BlockSpec(memory_space=pl.ANY)] * 4,
+        scratch_shapes=[pltpu.SemaphoreType.DMA((4,))],
+        name="write_results",
+    )(*[pltpu.with_memory_space_constraint(x, vmem) for x in outs])
     return outs[0], outs[1], outs[2].reshape(512), outs[3].reshape(512)
 
 

time: 40.6 us -> 35.7 us (0.88)
  the two profiles are of different devices: /device:TPU:1 before, /device:TPU:16 now
where the time goes in v2:
time: 35.7 us; the launch traced here: 35.5 us
  Pallas kernels  34.8 us (97%)
  between operations  0.65 us (2%)
    pallas_call x1, Pallas kernels, on_device(): pl.pallas_call(lambda *refs: step_kernel(n_region, n_dom, count, *refs),...  34.2 us

profile of v2, /device:TPU:16, one launch (start us, length us, event | category | flops | bytes accessed | tf_op | source)
XLA Modules:
  0.0 35.5 jit_solution(5105353639970384622)
XLA Ops:
  0.6 34.2 %newmark_step.1 = (f32[3,1024]{1,0:T(4,128)S(1)}, f32[3,1024]{1,0:T(4,128)S(1)}, f32[4,128]{1,0:T(4,128)S(1)}, f32[4,128]{1,0:T(4,128)S(1)}) custom-call(f32[3,1024]{1,0:T(4,128)} %refs_0_.1, f32[3,1024]{1,0:T(4,128)} %refs_1_.1, f32[3,1024]{1,0:T(4,128)} %refs_2_.1, s32[2,1024]{1,0:T(2,128)} %refs_3_.1, f32[3,2,1024]{2,1,0:T(2,128)} %refs_4_.1, ...), custom_call_target="tpu_custom_call" | custom-call | tf_op jit(solution)/shard_map/newmark_step/pallas_call | solution.py:469
  34.8 0.7 %write_results.1 = (f32[3,1024]{1,0:T(4,128)}, f32[3,1024]{1,0:T(4,128)}, f32[4,128]{1,0:T(4,128)}, f32[4,128]{1,0:T(4,128)}) custom-call(f32[3,1024]{1,0:T(4,128)S(1)} %get-tuple-element.12.refs_0_, f32[3,1024]{1,0:T(4,128)S(1)} %get-tuple-element.13.refs_1_, f32[4,128]{1,0:T(4,128)S(1)} %get-tuple-element.14.refs_2_, f32[4,128]{1,0:T(4,128)S(1)} %get-tuple-element.15.refs_3_), custom_call_target="tpu_custom_call" | custom-call | tf_op jit(solution)/shard_map/write_results/pallas_call | solution.py:503

commit v3 on v2

--- a/solution.py
+++ b/solution.py
@@ -136,8 +136,10 @@
         recv_sem,
         motion_send,
         motion_recv,
-        pressure_send,
-        pressure_recv,
+        slot_send,
+        slot_recv,
+        static_send,
+        static_recv,
         fluid_send,
         fluid_recv,
         solid_send,
@@ -182,22 +184,27 @@
     ) = held
 
     region, dom = lax.axis_index("region"), lax.axis_index("dom")
-    above = (lax.rem(region + 1, n_region), dom)
-    below = (lax.rem(region + n_region - 1, n_region), dom)
-    upper = (region, lax.rem(dom + 1, n_dom))
-    lower = (region, lax.rem(dom + n_dom - 1, n_dom))
-
     has_above, has_below = region < n_region - 1, region > 0
-    for ref in (motion_recv, pressure_recv):
+    to_region = {1: (has_above, has_below), -1: (has_below, has_above), 0: (None, None)}
+    device = {
+        (up, along): (
+            region + up,
+            lax.rem(dom + n_dom + along, n_dom),
+        )
+        for up in (-1, 0, 1)
+        for along in (-1, 0, 1)
+    }
+    for ref in (motion_recv, slot_recv, static_recv, fluid_recv):
         ref[...] = jnp.zeros(ref.shape, f32)
     barrier = pltpu.get_barrier_semaphore()
-    for held_if, other in ((has_above, above), (has_below, below), (None, upper), (None, lower)):
-        when(
-            held_if,
-            lambda other=other: pl.semaphore_signal(
-                barrier, inc=1, device_id=other, device_id_type=MESH
-            ),
-        )
+    for (up, along), other in device.items():
+        if (up, along) != (0, 0):
+            when(
+                to_region[up][0],
+                lambda other=other: pl.semaphore_signal(
+                    barrier, inc=1, device_id=other, device_id_type=MESH
+                ),
+            )
     loads = [
         pltpu.make_async_copy(source, target, load_sem.at[i])
         for i, (source, target) in enumerate(zip(sources, held))
@@ -205,26 +212,28 @@
     for load in loads:
         load.start()
 
-    def send(send_ref, recv_ref, flow, to_higher, to_lower, conditions=(None, None)):
+    started = []
+
+    def send(*messages):
         copies = []
-        for side, target in ((0, to_higher), (1, to_lower)):
+        for source, target, up, along in messages:
+            number = len(started)
             copy = pltpu.make_async_remote_copy(
-                src_ref=send_ref.at[side],
-                dst_ref=recv_ref.at[side],
-                send_sem=send_sem.at[2 * flow + side],
-                recv_sem=recv_sem.at[2 * flow + side],
-                device_id=target,
+                src_ref=source,
+                dst_ref=target,
+                send_sem=send_sem.at[number],
+                recv_sem=recv_sem.at[number],
+                device_id=device[up, along],
                 device_id_type=MESH,
             )
-            when(conditions[side], copy.start)
-            copies.append((copy, conditions[side], conditions[1 - side]))
+            when(to_region[up][0], copy.start)
+            started.append((copy, to_region[up][0]))
+            copies.append((copy, to_region[up][1]))
         return copies
 
     def receive(copies):
-        for copy, _, condition in copies:
+        for copy, condition in copies:
             when(condition, copy.wait_recv)
-
-    ends = (has_above, has_below)
 
     for i in range(5):
         loads[i].wait()
@@ -240,10 +249,13 @@
     motion = normals[0] * moved[0] + normals[1] * moved[1] + normals[2] * moved[2]
     motion_send[0] = motion[8:]
     motion_send[1] = motion[:8]
-    peers = 2 + lax.div(region + n_region - 1, n_region)
-    peers = peers + lax.div(2 * n_region - 2 - region, n_region)
+    peers = 2 + 3 * lax.div(region + n_region - 1, n_region)
+    peers = peers + 3 * lax.div(2 * n_region - 2 - region, n_region)
     pl.semaphore_wait(barrier, peers)
-    motion_copies = send(motion_send, motion_recv, 0, above, below, ends)
+    motion_copies = send(
+        (motion_send.at[0], motion_recv.at[0], 1, 0),
+        (motion_send.at[1], motion_recv.at[1], -1, 0),
+    )
 
     for i in range(5, 14):
         loads[i].wait()
@@ -277,29 +289,10 @@
     spread_high(fluid_terms, fluid_hi, [element])
     fluid_force = collect(fluid_terms, fluid_marks)[0]
 
-    for i in range(14, 17):
-        loads[i].wait()
-    fluid_slots = both_sides(fluid_interface)
-    arrived_hi, arrived_lo = fluid_slots >> 7, fluid_slots & 127
-    mark_low(arrived_marks, arrived_lo)
-    receive(motion_copies)
-    spread_high(
-        arrived_terms, arrived_hi, [jnp.concatenate([motion_recv[0], motion_recv[1]], axis=0)]
-    )
-    fluid_total = fluid_force + collect(arrived_terms, arrived_marks)[0]
-
     def rim_index(halo_ref, pad_ref, count):
         pad_ref[...] = jnp.full(pad_ref.shape, -1, jnp.int32)
         pad_ref[0:2, :count] = halo_ref[...]
         return pad_ref[...]
-
-    fluid_rim = rim_index(fluid_halo, index_pad.at[0:8], 48)
-    rim_values = lookup(
-        [[fluid_total[h : h + 1] for h in range(4)]], fluid_rim >> 7, fluid_rim & 127
-    )[0]
-    fluid_send[0] = rim_values[1:2]
-    fluid_send[1] = rim_values[0:1]
-    fluid_copies = send(fluid_send, fluid_recv, 1, upper, lower)
 
     def slot_of_node(rim):
         out = []
@@ -312,21 +305,57 @@
                 jnp.broadcast_to(line & 127, (LANES, LANES)) == marks_lane, 1.0, 0.0
             ).astype(bf16)
             terms = jnp.where(jnp.broadcast_to(line >> 7, (8, LANES)) == sublane, number, 0.0)
-            out.append(dot(terms.astype(bf16), marks, ((1,), (1,))).astype(jnp.int32) - 1)
+            out.append(dot(terms.astype(bf16), marks, ((1,), (1,))))
         return out
 
-    def add_rims(total, arrived, places):
-        for line, place in zip(arrived, places):
-            picked = jnp.take_along_axis(
-                jnp.broadcast_to(line, place.shape),
-                jnp.maximum(place, 0),
-                axis=1,
-                mode="promise_in_bounds",
-            )
-            total = total + jnp.where(place >= 0, picked, 0.0)
-        return total
-
+    def pick(line, place):
+        index = jnp.maximum(place.astype(jnp.int32) - 1, 0)
+        wide = jnp.broadcast_to(line, place.shape)
+        picked = jnp.take_along_axis(wide, index, axis=1, mode="promise_in_bounds")
+        return jnp.where(place > 0.5, picked, 0.0)
+
+    for i in range(14, 17):
+        loads[i].wait()
+    fluid_slots = both_sides(fluid_interface)
+    arrived_hi, arrived_lo = fluid_slots >> 7, fluid_slots & 127
+    fluid_rim = rim_index(fluid_halo, index_pad.at[0:8], 48)
     fluid_places = slot_of_node(fluid_rim)
+    slot_mass = lookup(
+        [[fluid_mass_inverse[h : h + 1] for h in range(4)]]
+        + [[place[h : h + 1] for h in range(4)] for place in fluid_places],
+        arrived_hi,
+        arrived_lo,
+    )
+    for i in range(3):
+        static_send[0, 8 * i : 8 * i + 8] = slot_mass[i][8:]
+        static_send[1, 8 * i : 8 * i + 8] = slot_mass[i][:8]
+    static_copies = send(
+        (static_send.at[0], static_recv.at[0], 1, 0),
+        (static_send.at[1], static_recv.at[1], -1, 0),
+    )
+    mark_low(arrived_marks, arrived_lo)
+    receive(motion_copies)
+    spread_high(
+        arrived_terms, arrived_hi, [jnp.concatenate([motion_recv[0], motion_recv[1]], axis=0)]
+    )
+    fluid_total = fluid_force + collect(arrived_terms, arrived_marks)[0]
+
+    total_rows = [[fluid_total[h : h + 1] for h in range(4)]]
+    at_slots = lookup(total_rows, arrived_hi, arrived_lo)[0]
+    slot_send[0] = at_slots[8:]
+    slot_send[1] = at_slots[:8]
+    rim_values = lookup(total_rows, fluid_rim >> 7, fluid_rim & 127)[0]
+    fluid_send[0] = rim_values[1:2]
+    fluid_send[1] = rim_values[0:1]
+    rim_copies = [
+        send(*((fluid_send.at[i], fluid_recv.at[i, 1 + up], up, 1 - 2 * i) for i in range(2)))
+        for up in (1, -1)
+    ]
+    slot_copies = send(
+        (slot_send.at[0], slot_recv.at[0], 1, 0),
+        (slot_send.at[1], slot_recv.at[1], -1, 0),
+    )
+    fluid_copies = send(*((fluid_send.at[i], fluid_recv.at[i, 1], 0, 1 - 2 * i) for i in range(2)))
 
     for i in range(17, 23):
         loads[i].wait()
@@ -358,22 +387,29 @@
     mark_low(element_marks, lo)
     spread_high(element_terms, hi, [element[32 * c : 32 * c + 32] for c in range(3)])
 
-    receive(fluid_copies)
-    assembled = add_rims(fluid_total, [fluid_recv[0], fluid_recv[1]], fluid_places)
-    ddot = fluid_mass_inverse[...] * assembled[:4]
-    pressure = lookup([[ddot[h : h + 1] for h in range(4)]], arrived_hi, arrived_lo)[0]
-    pressure_send[0] = pressure[8:]
-    pressure_send[1] = pressure[:8]
-    pressure_copies = send(pressure_send, pressure_recv, 2, above, below, ends)
-    ddot_out[...] = ddot
-    dot_out[...] = potential_dot[...] + 0.5 * time_step * (potential_ddot[...] + ddot)
-
     force = collect(element_terms, element_marks)
     mark_low(slot_marks, slot_lo)
     solid_rim = rim_index(solid_halo, index_pad.at[0:8], 96)
     solid_places = slot_of_node(solid_rim)
-    receive(pressure_copies)
-    arrived = jnp.concatenate([pressure_recv[0], pressure_recv[1]], axis=0)
+
+    receive(fluid_copies)
+    assembled = fluid_total
+    for i in range(2):
+        assembled = assembled + pick(fluid_recv[i, 1], fluid_places[i])
+    ddot = fluid_mass_inverse[...] * assembled[:4]
+    ddot_out[...] = ddot
+    dot_out[...] = potential_dot[...] + 0.5 * time_step * (potential_ddot[...] + ddot)
+
+    receive(static_copies)
+    for copies in rim_copies:
+        receive(copies)
+    receive(slot_copies)
+    arrived = []
+    for i, source in ((0, 2), (1, 0)):
+        mass, below_place, above_place = (static_recv[i, 8 * j : 8 * j + 8] for j in range(3))
+        value = slot_recv[i] + pick(fluid_recv[0, source], below_place)
+        arrived.append(mass * (value + pick(fluid_recv[1, source], above_place)))
+    arrived = jnp.concatenate(arrived, axis=0)
     spread_high(slot_terms, slot_hi, [-(normal * arrived) for normal in normals])
     coupling = collect(slot_terms, slot_marks)
     total = [a + b for a, b in zip(force, coupling)]
@@ -383,7 +419,10 @@
     for c in range(3):
         solid_send[0, c : c + 1] = rim_values[c][1:2]
         solid_send[1, c : c + 1] = rim_values[c][0:1]
-    solid_copies = send(solid_send, solid_recv, 3, upper, lower)
+    solid_copies = send(
+        (solid_send.at[0], solid_recv.at[0], 0, 1),
+        (solid_send.at[1], solid_recv.at[1], 0, -1),
+    )
     mass = solid_mass_inverse[...]
     base = [
         rows_of(velocity, (slice(c, c + 1), slice(None)))
@@ -392,13 +431,15 @@
     ]
     receive(solid_copies)
     for c in range(3):
-        arrived = [solid_recv[side, c : c + 1] for side in range(2)]
-        new = mass * add_rims(total[c], arrived, solid_places)
+        assembled = total[c]
+        for side in range(2):
+            assembled = assembled + pick(solid_recv[side, c : c + 1], solid_places[side])
+        new = mass * assembled
         speed = base[c] + 0.5 * time_step * new
         for h in range(8):
             acceleration_out[c : c + 1, LANES * h : LANES * (h + 1)] = new[h : h + 1]
             velocity_out[c : c + 1, LANES * h : LANES * (h + 1)] = speed[h : h + 1]
-    for copy, condition, _ in motion_copies + fluid_copies + pressure_copies + solid_copies:
+    for copy, condition in started:
         when(condition, copy.wait_send)
 
 
@@ -474,14 +515,16 @@
         scratch_shapes=[vmem(x.shape, x.dtype) for x in operands]
         + [
             pltpu.SemaphoreType.DMA((count,)),
-            pltpu.SemaphoreType.DMA((8,)),
-            pltpu.SemaphoreType.DMA((8,)),
+            pltpu.SemaphoreType.DMA((14,)),
+            pltpu.SemaphoreType.DMA((14,)),
             vmem((2, 8, LANES), f32),
             vmem((2, 8, LANES), f32),
             vmem((2, 8, LANES), f32),
             vmem((2, 8, LANES), f32),
+            vmem((2, 24, LANES), f32),
+            vmem((2, 24, LANES), f32),
             vmem((2, 1, LANES), f32),
-            vmem((2, 1, LANES), f32),
+            vmem((2, 3, 1, LANES), f32),
             vmem((2, 3, LANES), f32),
             vmem((2, 3, LANES), f32),
             vmem((32, LANES), jnp.int32),

time: 35.7 us -> 35 us (0.980)
  Pallas kernels: 34.8 us -> 34.1 us
    pallas_call x1, Pallas kernels: 34.2 us -> 33.4 us  [on_device(): pl.pallas_call(lambda *refs: step_kernel(n_region, n_dom, count, *refs),...]
where the time goes in v3:
time: 35 us; the launch traced here: 34.7 us
  Pallas kernels  34.1 us (97%)
  between operations  0.65 us (2%)
    pallas_call x1, Pallas kernels, on_device(): pl.pallas_call(lambda *refs: step_kernel(n_region, n_dom, count, *refs),...  33.4 us

profile of v3, /device:TPU:16, one launch (start us, length us, event | category | flops | bytes accessed | tf_op | source)
XLA Modules:
  0.0 34.7 jit_solution(2216503554966060954)
XLA Ops:
  0.6 33.4 %newmark_step.1 = (f32[3,1024]{1,0:T(4,128)S(1)}, f32[3,1024]{1,0:T(4,128)S(1)}, f32[4,128]{1,0:T(4,128)S(1)}, f32[4,128]{1,0:T(4,128)S(1)}) custom-call(f32[3,1024]{1,0:T(4,128)} %refs_0_.1, f32[3,1024]{1,0:T(4,128)} %refs_1_.1, f32[3,1024]{1,0:T(4,128)} %refs_2_.1, s32[2,1024]{1,0:T(2,128)} %refs_3_.1, f32[3,2,1024]{2,1,0:T(2,128)} %refs_4_.1, ...), custom_call_target="tpu_custom_call" | custom-call | tf_op jit(solution)/shard_map/newmark_step/pallas_call | solution.py:510
  34.1 0.7 %write_results.1 = (f32[3,1024]{1,0:T(4,128)}, f32[3,1024]{1,0:T(4,128)}, f32[4,128]{1,0:T(4,128)}, f32[4,128]{1,0:T(4,128)}) custom-call(f32[3,1024]{1,0:T(4,128)S(1)} %get-tuple-element.12.refs_0_, f32[3,1024]{1,0:T(4,128)S(1)} %get-tuple-element.13.refs_1_, f32[4,128]{1,0:T(4,128)S(1)} %get-tuple-element.14.refs_2_, f32[4,128]{1,0:T(4,128)S(1)} %get-tuple-element.15.refs_3_), custom_call_target="tpu_custom_call" | custom-call | tf_op jit(solution)/shard_map/write_results/pallas_call | solution.py:546

commit v4 on v3

--- a/solution.py
+++ b/solution.py
@@ -115,6 +115,21 @@
     ]
 
 
+def spread_rows(terms_ref, values):
+    sublane = lax.broadcasted_iota(jnp.int32, (8, LANES), 0)
+    for c, value in enumerate(values):
+        high = value.astype(bf16).astype(f32)
+        pair = (high, value - high)
+        for row in range(value.shape[0]):
+            first = row // 8 * 8
+            both = [
+                jnp.where(sublane == row % 8, part[first : first + 8], 0.0) for part in pair
+            ]
+            terms_ref[16 * c : 16 * c + 16, row * LANES : (row + 1) * LANES] = jnp.concatenate(
+                both, axis=0
+            ).astype(bf16)
+
+
 def rows_of(ref, lead):
     line = ref[lead]
     return jnp.concatenate([line[:, LANES * t : LANES * (t + 1)] for t in range(8)], axis=0)
@@ -136,14 +151,17 @@
         recv_sem,
         motion_send,
         motion_recv,
-        slot_send,
-        slot_recv,
         static_send,
         static_recv,
+        normals_send,
+        normals_recv,
+        rims_send,
+        rims_recv,
+        block_send,
+        block_recv,
         fluid_send,
         fluid_recv,
-        solid_send,
-        solid_recv,
+        far_recv,
         index_pad,
         field_pad,
         fluid_index_pad,
@@ -156,6 +174,8 @@
         slot_marks,
         arrived_terms,
         arrived_marks,
+        near_terms,
+        near_marks,
     ) = refs[2 * n_inputs + 4 :]
     (
         displacement,
@@ -192,13 +212,13 @@
             lax.rem(dom + n_dom + along, n_dom),
         )
         for up in (-1, 0, 1)
-        for along in (-1, 0, 1)
+        for along in (-2, -1, 0, 1, 2)
     }
-    for ref in (motion_recv, slot_recv, static_recv, fluid_recv):
+    for ref in (motion_recv, static_recv, block_recv, far_recv):
         ref[...] = jnp.zeros(ref.shape, f32)
     barrier = pltpu.get_barrier_semaphore()
     for (up, along), other in device.items():
-        if (up, along) != (0, 0):
+        if up != 0 or along in (-1, 1):
             when(
                 to_region[up][0],
                 lambda other=other: pl.semaphore_signal(
@@ -249,13 +269,6 @@
     motion = normals[0] * moved[0] + normals[1] * moved[1] + normals[2] * moved[2]
     motion_send[0] = motion[8:]
     motion_send[1] = motion[:8]
-    peers = 2 + 3 * lax.div(region + n_region - 1, n_region)
-    peers = peers + 3 * lax.div(2 * n_region - 2 - region, n_region)
-    pl.semaphore_wait(barrier, peers)
-    motion_copies = send(
-        (motion_send.at[0], motion_recv.at[0], 1, 0),
-        (motion_send.at[1], motion_recv.at[1], -1, 0),
-    )
 
     for i in range(5, 14):
         loads[i].wait()
@@ -329,35 +342,36 @@
     for i in range(3):
         static_send[0, 8 * i : 8 * i + 8] = slot_mass[i][8:]
         static_send[1, 8 * i : 8 * i + 8] = slot_mass[i][:8]
+    loads[21].wait()
+    solid_rim = rim_index(solid_halo, index_pad.at[0:8], 96)
+    solid_places = slot_of_node(solid_rim)
+    slot_places = lookup(
+        [[place[h : h + 1] for h in range(8)] for place in solid_places], slot_hi, slot_lo
+    )
+    for side in range(2):
+        for c in range(3):
+            normals_send[side, 16 * c : 16 * c + 16] = -normals[c]
+        normals_send[side, 48:] = slot_places[1 - side]
+
+    peers = 2 + 5 * lax.div(region + n_region - 1, n_region)
+    peers = peers + 5 * lax.div(2 * n_region - 2 - region, n_region)
+    pl.semaphore_wait(barrier, peers)
+    motion_copies = send(
+        (motion_send.at[0], motion_recv.at[0], 1, 0),
+        (motion_send.at[1], motion_recv.at[1], -1, 0),
+    )
+    normals_copies = send(
+        *((normals_send.at[i], normals_recv.at[i], 0, 1 - 2 * i) for i in range(2))
+    )
     static_copies = send(
-        (static_send.at[0], static_recv.at[0], 1, 0),
-        (static_send.at[1], static_recv.at[1], -1, 0),
-    )
-    mark_low(arrived_marks, arrived_lo)
-    receive(motion_copies)
-    spread_high(
-        arrived_terms, arrived_hi, [jnp.concatenate([motion_recv[0], motion_recv[1]], axis=0)]
-    )
-    fluid_total = fluid_force + collect(arrived_terms, arrived_marks)[0]
-
-    total_rows = [[fluid_total[h : h + 1] for h in range(4)]]
-    at_slots = lookup(total_rows, arrived_hi, arrived_lo)[0]
-    slot_send[0] = at_slots[8:]
-    slot_send[1] = at_slots[:8]
-    rim_values = lookup(total_rows, fluid_rim >> 7, fluid_rim & 127)[0]
-    fluid_send[0] = rim_values[1:2]
-    fluid_send[1] = rim_values[0:1]
-    rim_copies = [
-        send(*((fluid_send.at[i], fluid_recv.at[i, 1 + up], up, 1 - 2 * i) for i in range(2)))
-        for up in (1, -1)
-    ]
-    slot_copies = send(
-        (slot_send.at[0], slot_recv.at[0], 1, 0),
-        (slot_send.at[1], slot_recv.at[1], -1, 0),
-    )
-    fluid_copies = send(*((fluid_send.at[i], fluid_recv.at[i, 1], 0, 1 - 2 * i) for i in range(2)))
-
-    for i in range(17, 23):
+        *(
+            (static_send.at[i], static_recv.at[i, 1 + along], 1 - 2 * i, along)
+            for along in (-1, 0, 1)
+            for i in range(2)
+        )
+    )
+
+    for i in (17, 18, 19, 20, 22):
         loads[i].wait()
     index_pad[...] = jnp.full(index_pad.shape, -1, jnp.int32)
     index_pad[:, :125] = connectivity[...]
@@ -388,52 +402,103 @@
     spread_high(element_terms, hi, [element[32 * c : 32 * c + 32] for c in range(3)])
 
     force = collect(element_terms, element_marks)
+    rim_values = lookup(
+        [[t[h : h + 1] for h in range(8)] for t in force], solid_rim >> 7, solid_rim & 127
+    )
+    for c in range(3):
+        rims_send[0, c : c + 1] = rim_values[c][1:2]
+        rims_send[1, c : c + 1] = rim_values[c][0:1]
+    rims_copies = send(*((rims_send.at[i], rims_recv.at[i], 0, 1 - 2 * i) for i in range(2)))
+    mark_low(arrived_marks, arrived_lo)
+
+    receive(motion_copies)
+    spread_high(
+        arrived_terms, arrived_hi, [jnp.concatenate([motion_recv[0], motion_recv[1]], axis=0)]
+    )
+    fluid_total = fluid_force + collect(arrived_terms, arrived_marks)[0]
+    total_rows = [[fluid_total[h : h + 1] for h in range(4)]]
+    at_slots = lookup(total_rows, arrived_hi, arrived_lo)[0]
+    rim_values = lookup(total_rows, fluid_rim >> 7, fluid_rim & 127)[0]
+    for i in range(2):
+        block_send[i, :8] = at_slots[8 - 8 * i : 16 - 8 * i]
+        block_send[i, 8:9] = rim_values[1:2]
+        block_send[i, 9:10] = rim_values[0:1]
+        fluid_send[i] = rim_values[1 - i : 2 - i]
+    block_copies = send(
+        *(
+            (block_send.at[i], block_recv.at[i, 1 + along], 1 - 2 * i, along)
+            for along in (-1, 1, 0)
+            for i in range(2)
+        ),
+        *(
+            (fluid_send.at[j], far_recv.at[i, j], 1 - 2 * i, 2 - 4 * j)
+            for j in range(2)
+            for i in range(2)
+        ),
+    )
+    fluid_copies = send(*((fluid_send.at[i], fluid_recv.at[i], 0, 1 - 2 * i) for i in range(2)))
+
     mark_low(slot_marks, slot_lo)
-    solid_rim = rim_index(solid_halo, index_pad.at[0:8], 96)
-    solid_places = slot_of_node(solid_rim)
-
-    receive(fluid_copies)
-    assembled = fluid_total
+    receive(normals_copies)
     for i in range(2):
-        assembled = assembled + pick(fluid_recv[i, 1], fluid_places[i])
-    ddot = fluid_mass_inverse[...] * assembled[:4]
-    ddot_out[...] = ddot
-    dot_out[...] = potential_dot[...] + 0.5 * time_step * (potential_ddot[...] + ddot)
-
-    receive(static_copies)
-    for copies in rim_copies:
-        receive(copies)
-    receive(slot_copies)
-    arrived = []
-    for i, source in ((0, 2), (1, 0)):
-        mass, below_place, above_place = (static_recv[i, 8 * j : 8 * j + 8] for j in range(3))
-        value = slot_recv[i] + pick(fluid_recv[0, source], below_place)
-        arrived.append(mass * (value + pick(fluid_recv[1, source], above_place)))
-    arrived = jnp.concatenate(arrived, axis=0)
-    spread_high(slot_terms, slot_hi, [-(normal * arrived) for normal in normals])
-    coupling = collect(slot_terms, slot_marks)
-    total = [a + b for a, b in zip(force, coupling)]
-    rim_values = lookup(
-        [[t[h : h + 1] for h in range(8)] for t in total], solid_rim >> 7, solid_rim & 127
-    )
-    for c in range(3):
-        solid_send[0, c : c + 1] = rim_values[c][1:2]
-        solid_send[1, c : c + 1] = rim_values[c][0:1]
-    solid_copies = send(
-        (solid_send.at[0], solid_recv.at[0], 0, 1),
-        (solid_send.at[1], solid_recv.at[1], 0, -1),
-    )
+        mark_low(near_marks.at[i], normals_recv[i, 48:].astype(jnp.int32) - 1)
     mass = solid_mass_inverse[...]
     base = [
         rows_of(velocity, (slice(c, c + 1), slice(None)))
         + 0.5 * time_step * rows_of(acceleration, (slice(c, c + 1), slice(None)))
         for c in range(3)
     ]
-    receive(solid_copies)
+    receive(fluid_copies)
+    assembled = fluid_total
+    for i in range(2):
+        assembled = assembled + pick(fluid_recv[i], fluid_places[i])
+    ddot = fluid_mass_inverse[...] * assembled[:4]
+    ddot_out[...] = ddot
+    dot_out[...] = potential_dot[...] + 0.5 * time_step * (potential_ddot[...] + ddot)
+    receive(static_copies)
+    receive(rims_copies)
+
+    receive(block_copies)
+
+    def pressure_of(column):
+        sides = []
+        for i in range(2):
+            block = block_recv.at[i, 1 - column]
+            if column == -1:
+                low_rim = far_recv[i, 0]
+            else:
+                low_rim = block_recv[i, 2 - column, 8:9]
+            if column == 1:
+                high_rim = far_recv[i, 1]
+            else:
+                high_rim = block_recv[i, -column, 9:10]
+            slot_mass, low_place, high_place = (
+                static_recv[i, 1 - column, 8 * j : 8 * j + 8] for j in range(3)
+            )
+            value = block[:8] + pick(low_rim, low_place)
+            sides.append(slot_mass * (value + pick(high_rim, high_place)))
+        return jnp.concatenate(sides, axis=0)
+
+    arrived = pressure_of(0)
+    spread_high(slot_terms, slot_hi, [-(normal * arrived) for normal in normals])
+    for i in range(2):
+        arrived = pressure_of(2 * i - 1)
+        spread_rows(
+            near_terms.at[i],
+            [normals_recv[i, 16 * c : 16 * c + 16] * arrived for c in range(3)],
+        )
+    coupling = collect(slot_terms, slot_marks)
+    near = []
+    for i in range(2):
+        sums = dot(near_terms[i], near_marks[i], ((1,), (1,)))
+        near.append(
+            [jnp.sum(sums[16 * c : 16 * c + 16], axis=0, keepdims=True) for c in range(3)]
+        )
     for c in range(3):
-        assembled = total[c]
-        for side in range(2):
-            assembled = assembled + pick(solid_recv[side, c : c + 1], solid_places[side])
+        assembled = force[c] + coupling[c]
+        for i in range(2):
+            line = rims_recv[i, c : c + 1] + near[i][c]
+            assembled = assembled + pick(line, solid_places[i])
         new = mass * assembled
         speed = base[c] + 0.5 * time_step * new
         for h in range(8):
@@ -515,18 +580,21 @@
         scratch_shapes=[vmem(x.shape, x.dtype) for x in operands]
         + [
             pltpu.SemaphoreType.DMA((count,)),
-            pltpu.SemaphoreType.DMA((14,)),
-            pltpu.SemaphoreType.DMA((14,)),
-            vmem((2, 8, LANES), f32),
-            vmem((2, 8, LANES), f32),
+            pltpu.SemaphoreType.DMA((24,)),
+            pltpu.SemaphoreType.DMA((24,)),
             vmem((2, 8, LANES), f32),
             vmem((2, 8, LANES), f32),
             vmem((2, 24, LANES), f32),
-            vmem((2, 24, LANES), f32),
-            vmem((2, 1, LANES), f32),
-            vmem((2, 3, 1, LANES), f32),
+            vmem((2, 3, 24, LANES), f32),
+            vmem((2, 64, LANES), f32),
+            vmem((2, 64, LANES), f32),
             vmem((2, 3, LANES), f32),
             vmem((2, 3, LANES), f32),
+            vmem((2, 16, LANES), f32),
+            vmem((2, 3, 16, LANES), f32),
+            vmem((2, 1, LANES), f32),
+            vmem((2, 1, LANES), f32),
+            vmem((2, 2, 1, LANES), f32),
             vmem((32, LANES), jnp.int32),
             vmem((32, LANES), f32),
             vmem((16, LANES), jnp.int32),
@@ -539,6 +607,8 @@
             vmem((LANES, 16 * LANES), bf16),
             vmem((16, 16 * LANES), bf16),
             vmem((LANES, 16 * LANES), bf16),
+            vmem((2, 48, 16 * LANES), bf16),
+            vmem((2, LANES, 16 * LANES), bf16),
         ],
         compiler_params=pltpu.CompilerParams(collective_id=0, has_side_effects=True),
         name="newmark_step",

time: 35 us -> 32.7 us (0.934)
  the two profiles are of different devices: /device:TPU:16 before, /device:TPU:6 now
where the time goes in v4:
time: 32.7 us; the launch traced here: 32.5 us
  Pallas kernels  31.8 us (97%)
  between operations  0.65 us (2%)
    pallas_call x1, Pallas kernels, on_device(): pl.pallas_call(lambda *refs: step_kernel(n_region, n_dom, count, *refs),...  31.2 us

profile of v4, /device:TPU:6, one launch (start us, length us, event | category | flops | bytes accessed | tf_op | source)
XLA Modules:
  0.0 32.5 jit_solution(12215490364832950285)
XLA Ops:
  0.6 31.2 %newmark_step.1 = (f32[3,1024]{1,0:T(4,128)S(1)}, f32[3,1024]{1,0:T(4,128)S(1)}, f32[4,128]{1,0:T(4,128)S(1)}, f32[4,128]{1,0:T(4,128)S(1)}) custom-call(f32[3,1024]{1,0:T(4,128)} %refs_0_.1, f32[3,1024]{1,0:T(4,128)} %refs_1_.1, f32[3,1024]{1,0:T(4,128)} %refs_2_.1, s32[2,1024]{1,0:T(2,128)} %refs_3_.1, f32[3,2,1024]{2,1,0:T(2,128)} %refs_4_.1, ...), custom_call_target="tpu_custom_call" | custom-call | tf_op jit(solution)/shard_map/newmark_step/pallas_call | solution.py:575
  31.8 0.7 %write_results.1 = (f32[3,1024]{1,0:T(4,128)}, f32[3,1024]{1,0:T(4,128)}, f32[4,128]{1,0:T(4,128)}, f32[4,128]{1,0:T(4,128)}) custom-call(f32[3,1024]{1,0:T(4,128)S(1)} %get-tuple-element.12.refs_0_, f32[3,1024]{1,0:T(4,128)S(1)} %get-tuple-element.13.refs_1_, f32[4,128]{1,0:T(4,128)S(1)} %get-tuple-element.14.refs_2_, f32[4,128]{1,0:T(4,128)S(1)} %get-tuple-element.15.refs_3_), custom_call_target="tpu_custom_call" | custom-call | tf_op jit(solution)/shard_map/write_results/pallas_call | solution.py:616

commit v5 on v4

--- a/solution.py
+++ b/solution.py
@@ -107,8 +107,16 @@
             ).astype(bf16)
 
 
+def halved(terms_ref, marks_ref):
+    middle = terms_ref.shape[1] // 2
+    return sum(
+        dot(terms_ref[:, half], marks_ref[:, half], ((1,), (1,)))
+        for half in (slice(0, middle), slice(middle, 2 * middle))
+    )
+
+
 def collect(terms_ref, marks_ref):
-    sums = dot(terms_ref[...], marks_ref[...], ((1,), (1,)))
+    sums = halved(terms_ref, marks_ref)
     return [
         sums[16 * c : 16 * c + 8] + sums[16 * c + 8 : 16 * c + 16]
         for c in range(terms_ref.shape[0] // 16)
@@ -147,6 +155,8 @@
     held = refs[n_inputs + 4 : 2 * n_inputs + 4]
     (
         load_sem,
+        passed_sem,
+        known_sem,
         send_sem,
         recv_sem,
         motion_send,
@@ -218,7 +228,7 @@
         ref[...] = jnp.zeros(ref.shape, f32)
     barrier = pltpu.get_barrier_semaphore()
     for (up, along), other in device.items():
-        if up != 0 or along in (-1, 1):
+        if abs(up) + abs(along) == 1:
             when(
                 to_region[up][0],
                 lambda other=other: pl.semaphore_signal(
@@ -270,6 +280,22 @@
     motion_send[0] = motion[8:]
     motion_send[1] = motion[:8]
 
+    peers = 2 + lax.div(region + n_region - 1, n_region)
+    peers = peers + lax.div(2 * n_region - 2 - region, n_region)
+    pl.semaphore_wait(barrier, peers)
+
+    def greet(semaphore):
+        for along in (-1, 1):
+            pl.semaphore_signal(
+                semaphore, inc=1, device_id=device[0, along], device_id_type=MESH
+            )
+
+    greet(passed_sem)
+    motion_copies = send(
+        (motion_send.at[0], motion_recv.at[0], 1, 0),
+        (motion_send.at[1], motion_recv.at[1], -1, 0),
+    )
+
     for i in range(5, 14):
         loads[i].wait()
     fluid_predicted = (
@@ -353,13 +379,8 @@
             normals_send[side, 16 * c : 16 * c + 16] = -normals[c]
         normals_send[side, 48:] = slot_places[1 - side]
 
-    peers = 2 + 5 * lax.div(region + n_region - 1, n_region)
-    peers = peers + 5 * lax.div(2 * n_region - 2 - region, n_region)
-    pl.semaphore_wait(barrier, peers)
-    motion_copies = send(
-        (motion_send.at[0], motion_recv.at[0], 1, 0),
-        (motion_send.at[1], motion_recv.at[1], -1, 0),
-    )
+    pl.semaphore_wait(passed_sem, 2)
+    greet(known_sem)
     normals_copies = send(
         *((normals_send.at[i], normals_recv.at[i], 0, 1 - 2 * i) for i in range(2))
     )
@@ -411,6 +432,7 @@
     rims_copies = send(*((rims_send.at[i], rims_recv.at[i], 0, 1 - 2 * i) for i in range(2)))
     mark_low(arrived_marks, arrived_lo)
 
+    pl.semaphore_wait(known_sem, 2)
     receive(motion_copies)
     spread_high(
         arrived_terms, arrived_hi, [jnp.concatenate([motion_recv[0], motion_recv[1]], axis=0)]
@@ -426,13 +448,13 @@
         fluid_send[i] = rim_values[1 - i : 2 - i]
     block_copies = send(
         *(
-            (block_send.at[i], block_recv.at[i, 1 + along], 1 - 2 * i, along)
-            for along in (-1, 1, 0)
+            (fluid_send.at[j], far_recv.at[i, j], 1 - 2 * i, 2 - 4 * j)
+            for j in range(2)
             for i in range(2)
         ),
         *(
-            (fluid_send.at[j], far_recv.at[i, j], 1 - 2 * i, 2 - 4 * j)
-            for j in range(2)
+            (block_send.at[i], block_recv.at[i, 1 + along], 1 - 2 * i, along)
+            for along in (-1, 1, 0)
             for i in range(2)
         ),
     )
@@ -580,6 +602,8 @@
         scratch_shapes=[vmem(x.shape, x.dtype) for x in operands]
         + [
             pltpu.SemaphoreType.DMA((count,)),
+            pltpu.SemaphoreType.REGULAR,
+            pltpu.SemaphoreType.REGULAR,
             pltpu.SemaphoreType.DMA((24,)),
             pltpu.SemaphoreType.DMA((24,)),
             vmem((2, 8, LANES), f32),

time: 32.7 us -> 32.2 us (0.985)
  Pallas kernels: 31.8 us -> 31.4 us
    pallas_call x1, Pallas kernels: 31.2 us -> 30.7 us  [on_device(): pl.pallas_call(lambda *refs: step_kernel(n_region, n_dom, count, *refs),...]
where the time goes in v5:
time: 32.2 us; the launch traced here: 32 us
  Pallas kernels  31.4 us (98%)
  between operations  0.65 us (2%)
    pallas_call x1, Pallas kernels, on_device(): pl.pallas_call(lambda *refs: step_kernel(n_region, n_dom, count, *refs),...  30.7 us
    pallas_call x1, Pallas kernels, on_device(): pl.pallas_call(write_kernel, out_shape=tuple((jax.ShapeDtypeStruct(shape,...  0.65 us

profile of v5, /device:TPU:6, one launch (start us, length us, event | category | flops | bytes accessed | tf_op | source)
XLA Modules:
  0.0 32.0 jit_solution(4016399934505914744)
XLA Ops:
  0.6 30.7 %newmark_step.1 = (f32[3,1024]{1,0:T(4,128)S(1)}, f32[3,1024]{1,0:T(4,128)S(1)}, f32[4,128]{1,0:T(4,128)S(1)}, f32[4,128]{1,0:T(4,128)S(1)}) custom-call(f32[3,1024]{1,0:T(4,128)} %refs_0_.1, f32[3,1024]{1,0:T(4,128)} %refs_1_.1, f32[3,1024]{1,0:T(4,128)} %refs_2_.1, s32[2,1024]{1,0:T(2,128)} %refs_3_.1, f32[3,2,1024]{2,1,0:T(2,128)} %refs_4_.1, ...), custom_call_target="tpu_custom_call" | custom-call | tf_op jit(solution)/shard_map/newmark_step/pallas_call | solution.py:597
  31.4 0.7 %write_results.1 = (f32[3,1024]{1,0:T(4,128)}, f32[3,1024]{1,0:T(4,128)}, f32[4,128]{1,0:T(4,128)}, f32[4,128]{1,0:T(4,128)}) custom-call(f32[3,1024]{1,0:T(4,128)S(1)} %get-tuple-element.12.refs_0_, f32[3,1024]{1,0:T(4,128)S(1)} %get-tuple-element.13.refs_1_, f32[4,128]{1,0:T(4,128)S(1)} %get-tuple-element.14.refs_2_, f32[4,128]{1,0:T(4,128)S(1)} %get-tuple-element.15.refs_3_), custom_call_target="tpu_custom_call" | custom-call | tf_op jit(solution)/shard_map/write_results/pallas_call | solution.py:640

commit v6 on v5

--- a/solution.py
+++ b/solution.py
@@ -149,15 +149,14 @@
     )
 
 
-def step_kernel(n_region, n_dom, n_inputs, *refs):
+def step_kernel(n_region, n_dom, n_inputs, local, *refs):
+    load_sem, send_sem = local
     sources = refs[:n_inputs]
     velocity_out, acceleration_out, dot_out, ddot_out = refs[n_inputs : n_inputs + 4]
     held = refs[n_inputs + 4 : 2 * n_inputs + 4]
     (
-        load_sem,
         passed_sem,
         known_sem,
-        send_sem,
         recv_sem,
         motion_send,
         motion_recv,
@@ -595,16 +594,18 @@
     vmem = pltpu.VMEM
     shapes = ((3, 1024), (3, 1024), (4, LANES), (4, LANES))
     outs = pl.pallas_call(
-        lambda *refs: step_kernel(n_region, n_dom, count, *refs),
+        lambda *refs: pl.run_scoped(
+            lambda *local: step_kernel(n_region, n_dom, count, local, *refs),
+            pltpu.SemaphoreType.DMA((count,)),
+            pltpu.SemaphoreType.DMA((24,)),
+        ),
         out_shape=tuple(pltpu.VMEM(shape, f32) for shape in shapes),
         in_specs=[pl.BlockSpec(memory_space=pl.ANY)] * count,
         out_specs=[pl.BlockSpec(memory_space=vmem)] * 4,
         scratch_shapes=[vmem(x.shape, x.dtype) for x in operands]
         + [
-            pltpu.SemaphoreType.DMA((count,)),
             pltpu.SemaphoreType.REGULAR,
             pltpu.SemaphoreType.REGULAR,
-            pltpu.SemaphoreType.DMA((24,)),
             pltpu.SemaphoreType.DMA((24,)),
             vmem((2, 8, LANES), f32),
             vmem((2, 8, LANES), f32),

time: 32.2 us -> 31.8 us (0.988)
  Pallas kernels: 31.4 us -> 30.9 us
    pallas_call x1, Pallas kernels: 30.7 us -> 30.3 us  [on_device(): pl.pallas_call(lambda *refs: pl.run_scoped(lambda *local: step_kernel(n_r...]
where the time goes in v6:
time: 31.8 us; the launch traced here: 31.6 us
  Pallas kernels  30.9 us (97%)
  between operations  0.65 us (2%)
    pallas_call x1, Pallas kernels, on_device(): pl.pallas_call(lambda *refs: pl.run_scoped(lambda *local: step_kernel(n_r...  30.3 us
    pallas_call x1, Pallas kernels, on_device(): pl.pallas_call(write_kernel, out_shape=tuple((jax.ShapeDtypeStruct(shape,...  0.65 us

profile of v6, /device:TPU:6, one launch (start us, length us, event | category | flops | bytes accessed | tf_op | source)
XLA Modules:
  0.0 31.6 jit_solution(15707603753122654082)
XLA Ops:
  0.6 30.3 %newmark_step.1 = (f32[3,1024]{1,0:T(4,128)S(1)}, f32[3,1024]{1,0:T(4,128)S(1)}, f32[4,128]{1,0:T(4,128)S(1)}, f32[4,128]{1,0:T(4,128)S(1)}) custom-call(f32[3,1024]{1,0:T(4,128)} %refs_0_.1, f32[3,1024]{1,0:T(4,128)} %refs_1_.1, f32[3,1024]{1,0:T(4,128)} %refs_2_.1, s32[2,1024]{1,0:T(2,128)} %refs_3_.1, f32[3,2,1024]{2,1,0:T(2,128)} %refs_4_.1, ...), custom_call_target="tpu_custom_call" | custom-call | tf_op jit(solution)/shard_map/newmark_step/pallas_call | solution.py:596
  30.9 0.7 %write_results.1 = (f32[3,1024]{1,0:T(4,128)}, f32[3,1024]{1,0:T(4,128)}, f32[4,128]{1,0:T(4,128)}, f32[4,128]{1,0:T(4,128)}) custom-call(f32[3,1024]{1,0:T(4,128)S(1)} %get-tuple-element.12.refs_0_, f32[3,1024]{1,0:T(4,128)S(1)} %get-tuple-element.13.refs_1_, f32[4,128]{1,0:T(4,128)S(1)} %get-tuple-element.14.refs_2_, f32[4,128]{1,0:T(4,128)S(1)} %get-tuple-element.15.refs_3_), custom_call_target="tpu_custom_call" | custom-call | tf_op jit(solution)/shard_map/write_results/pallas_call | solution.py:641

commit v7 on v6

--- a/solution.py
+++ b/solution.py
@@ -81,9 +81,10 @@
 
 
 def mark_low(marks_ref, lo):
-    sublane = lax.broadcasted_iota(jnp.int32, (LANES, LANES), 0)
+    shape = (marks_ref.shape[0], LANES)
+    sublane = lax.broadcasted_iota(jnp.int32, shape, 0)
     for row in range(lo.shape[0]):
-        line = jnp.broadcast_to(lo[row : row + 1], (LANES, LANES))
+        line = jnp.broadcast_to(lo[row : row + 1], shape)
         marks_ref[:, row * LANES : (row + 1) * LANES] = jnp.where(line == sublane, 1.0, 0.0).astype(
             bf16
         )
@@ -508,17 +509,18 @@
             near_terms.at[i],
             [normals_recv[i, 16 * c : 16 * c + 16] * arrived for c in range(3)],
         )
-    coupling = collect(slot_terms, slot_marks)
+    blank = jnp.zeros((1, LANES - 96), f32)
     near = []
     for i in range(2):
         sums = dot(near_terms[i], near_marks[i], ((1,), (1,)))
         near.append(
             [jnp.sum(sums[16 * c : 16 * c + 16], axis=0, keepdims=True) for c in range(3)]
         )
+    coupling = collect(slot_terms, slot_marks)
     for c in range(3):
         assembled = force[c] + coupling[c]
         for i in range(2):
-            line = rims_recv[i, c : c + 1] + near[i][c]
+            line = rims_recv[i, c : c + 1] + jnp.concatenate([near[i][c], blank], axis=1)
             assembled = assembled + pick(line, solid_places[i])
         new = mass * assembled
         speed = base[c] + 0.5 * time_step * new
@@ -633,7 +635,7 @@
             vmem((16, 16 * LANES), bf16),
             vmem((LANES, 16 * LANES), bf16),
             vmem((2, 48, 16 * LANES), bf16),
-            vmem((2, LANES, 16 * LANES), bf16),
+            vmem((2, 96, 16 * LANES), bf16),
         ],
         compiler_params=pltpu.CompilerParams(collective_id=0, has_side_effects=True),
         name="newmark_step",

time: 31.8 us -> 31.7 us (level)
  no operation moved by 1% of the time
where the time goes in v7:
time: 31.7 us; the launch traced here: 31.5 us
  Pallas kernels  30.8 us (97%)
  between operations  0.65 us (2%)
    pallas_call x1, Pallas kernels, on_device(): pl.pallas_call(lambda *refs: pl.run_scoped(lambda *local: step_kernel(n_r...  30.2 us
    pallas_call x1, Pallas kernels, on_device(): pl.pallas_call(write_kernel, out_shape=tuple((jax.ShapeDtypeStruct(shape,...  0.65 us

profile of v7, /device:TPU:6, one launch (start us, length us, event | category | flops | bytes accessed | tf_op | source)
XLA Modules:
  0.0 31.5 jit_solution(11008388172958953724)
XLA Ops:
  0.6 30.2 %newmark_step.1 = (f32[3,1024]{1,0:T(4,128)S(1)}, f32[3,1024]{1,0:T(4,128)S(1)}, f32[4,128]{1,0:T(4,128)S(1)}, f32[4,128]{1,0:T(4,128)S(1)}) custom-call(f32[3,1024]{1,0:T(4,128)} %refs_0_.1, f32[3,1024]{1,0:T(4,128)} %refs_1_.1, f32[3,1024]{1,0:T(4,128)} %refs_2_.1, s32[2,1024]{1,0:T(2,128)} %refs_3_.1, f32[3,2,1024]{2,1,0:T(2,128)} %refs_4_.1, ...), custom_call_target="tpu_custom_call" | custom-call | tf_op jit(solution)/shard_map/newmark_step/pallas_call | solution.py:598
  30.8 0.7 %write_results.1 = (f32[3,1024]{1,0:T(4,128)}, f32[3,1024]{1,0:T(4,128)}, f32[4,128]{1,0:T(4,128)}, f32[4,128]{1,0:T(4,128)}) custom-call(f32[3,1024]{1,0:T(4,128)S(1)} %get-tuple-element.12.refs_0_, f32[3,1024]{1,0:T(4,128)S(1)} %get-tuple-element.13.refs_1_, f32[4,128]{1,0:T(4,128)S(1)} %get-tuple-element.14.refs_2_, f32[4,128]{1,0:T(4,128)S(1)} %get-tuple-element.15.refs_3_), custom_call_target="tpu_custom_call" | custom-call | tf_op jit(solution)/shard_map/write_results/pallas_call | solution.py:643
